TPU v7x, 512 devices: a whole 4x8x8 slice. The times are simulated.
512 devices in a mesh: group: 8 (over z), dom: 64 (over y, x, core).
Axes of the slice: x: 4, y: 8, z: 8, core: 2. Of those that a mesh axis runs over, the one named last changes fastest.
Arguments:
- orbitals: bfloat16 [1572864, 512], P(('group', 'dom')), may hold values from -6 to 6
- density_rows: bfloat16 [16384, 2048], P(('group', 'dom')), may hold values from -0.01171875 to 0.01171875
- near_blocks: int32 [512, 32], P(('group', 'dom')), may hold values from 0 to 127, as said below
- leaf_coords: int32 [3, 3072], P(None, ('group', 'dom')), may hold values from 0 to 127, as said below
- near_leaves: int32 [3072, 3], P(('group', 'dom')), may hold values from 0 to 17, as said below
- leaf_basis: float32 [64, 1572864], P(None, ('group', 'dom')), may hold values from -2 to 2
- leaf_transfer: float32 [3072, 64, 64], P(('group', 'dom')), may hold values from -0.75 to 0.75
- dev_transfer: float32 [512, 64, 64], P(('group', 'dom')), may hold values from -0.375 to 0.375
- dev_far: int32 [512, 64], P(('group', 'dom')), may hold values 0 or 1
- group_far: int32 [8, 8], P('group'), may hold values 0 or 1
Outputs:
- density: float32 [1572864], P(('group', 'dom'))
- hartree: float32 [1572864], P(('group', 'dom'))
Inputs may be any that keep to these rules, and one draw needn't show every extreme that they name: `near_blocks`: each row names 32 distinct blocks of its own coarse domain; block b is rows b * 16 to b * 16 + 15 of the domain's density matrix, held by the device of dom index b // 2. The first 2 entries of every row of a domain are the same: all blocks of one device of that domain, in order. Every other entry is a block held by a device whose dom index differs from the row's own by at most 8, counted cyclically over the 64 dom indices. `near_leaves`: each row names 3 distinct window positions, among them the leaf's own position 6 + (t mod 6) for row t. `leaf_coords`: distinct positions for all leaves.
All inputs are finite; a program needn't handle non-finite values. No bound on the sum of `dev_far` or of `group_far` on one device may be relied on, other than what follows from the above.
Results may differ from a plain program's by a relative error of at most 0.0003.
Values may be sent and summed in bfloat16 or wider, within the bound.
A program may use at most 128 MiB of HBM per device.

v0:
```python
import math

import jax
import jax.numpy as jnp
from jax import lax
from jax.sharding import PartitionSpec as P

SIDE = 8
LEAF = 512
CHEB = 4
BW = 16
NEARL = 3


vol_weight = 0.1
soft_square = 1.0


def with_halo(value, sides, width):
    for axis, dim in sides:
        peers, length = (lax.axis_size(axis), value.shape[dim])
        up = [(i, (i + 1) % peers) for i in range(peers - 1)]
        down = [(j, i) for i, j in up]
        last = lax.slice_in_dim(value, length - width, length, axis=dim)
        first = lax.slice_in_dim(value, 0, width, axis=dim)
        before = lax.ppermute(last, axis, up)
        after = lax.ppermute(first, axis, down)
        value = jnp.concatenate([before, value, after], axis=dim)
    return value


def coulomb(target, source):
    diff_x = target[0][:, None] - source[0][None, :]
    diff_y = target[1][:, None] - source[1][None, :]
    diff_z = target[2][:, None] - source[2][None, :]
    return 1.0 / jnp.sqrt(diff_x * diff_x + diff_y * diff_y + diff_z * diff_z + soft_square)


def cluster_nodes(bounds):
    steps_idx = jnp.arange(CHEB).astype(jnp.float32)
    cheb_points = jnp.cos((2.0 * steps_idx + 1.0) * (math.pi / (2.0 * CHEB)))
    centre = 0.5 * (bounds[:3] + bounds[3:])
    half_size = 0.5 * (bounds[3:] - bounds[:3])
    along = centre[:, None] + half_size[:, None] * cheb_points[None, :]
    node_index = jnp.arange(CHEB * CHEB * CHEB)
    first = node_index // (CHEB * CHEB)
    second = node_index // CHEB % CHEB
    third = node_index % CHEB
    return jnp.stack([along[0][first], along[1][second], along[2][third]])


def point_offsets():
    place = jnp.arange(LEAF)
    return jnp.stack([place // (SIDE * SIDE), place // SIDE % SIDE, place % SIDE]).astype(
        jnp.float32
    )


def far_coupling(own_nodes, other_bounds, mask_row, moments):
    other_nodes = jax.vmap(cluster_nodes)(other_bounds)
    coupling = jax.vmap(lambda other: coulomb(own_nodes, other))(other_nodes)
    coupling = coupling * mask_row.astype(jnp.float32)[:, None, None]
    return vol_weight * jnp.einsum("srq,sq->r", coupling, moments, precision=lax.Precision.HIGHEST)


def local(
    orbitals,
    density_rows,
    near_blocks,
    leaf_coords,
    near_leaves,
    leaf_basis,
    leaf_transfer,
    dev_transfer,
    dev_far,
    group_far,
):
    near_list = near_blocks[0]
    near_width = orbitals.shape[1]
    blocks_group = density_rows.shape[1] // BW
    rows_global = (near_list[:, None] * BW + jnp.arange(BW)[None, :]).reshape(-1)
    row_piece = lax.all_gather(density_rows, "dom", axis=0, tiled=True)
    piece_rows = row_piece.shape[0]
    columns = jnp.take(row_piece.reshape(piece_rows, blocks_group, BW), near_list, axis=1).reshape(
        piece_rows, near_width
    )
    inside = (rows_global >= 0) & (rows_global < piece_rows)
    chosen = jnp.take(columns, jnp.clip(rows_global, 0, piece_rows - 1), axis=0)
    local_matrix = jnp.where(
        inside[:, None], chosen, jnp.zeros((near_width, near_width), jnp.bfloat16)
    )
    product = jnp.dot(orbitals, local_matrix, preferred_element_type=jnp.float32)
    density = jnp.sum(product * orbitals.astype(jnp.float32), axis=1)
    leaf_count = leaf_coords.shape[1]
    coords_f = leaf_coords.astype(jnp.float32)
    points = SIDE * coords_f.T[:, :, None] + point_offsets()[None]
    rho_leaf = density.reshape(leaf_count, LEAF)
    packed = jnp.concatenate([points, rho_leaf[:, None, :]], axis=1)
    window = with_halo(packed, (("dom", 0),), leaf_count)

    def near_one(leaf_index):
        own_points = points[leaf_index]
        running = jnp.zeros((LEAF,), jnp.float32)
        for near_slot in range(NEARL):
            source_leaf = window[near_leaves[leaf_index, near_slot]]
            running = running + jnp.dot(
                coulomb(own_points, source_leaf[:3]),
                source_leaf[3],
                precision=lax.Precision.HIGHEST,
            )
        return running

    near_part = lax.map(near_one, jnp.arange(leaf_count)) * vol_weight
    rank = leaf_basis.shape[0]
    leaf_bases = leaf_basis.reshape(rank, leaf_count, LEAF)
    leaf_mom = jnp.einsum("rlp,lp->lr", leaf_bases, rho_leaf, precision=lax.Precision.HIGHEST)
    dev_mom = jnp.einsum("lqr,lq->r", leaf_transfer, leaf_mom, precision=lax.Precision.HIGHEST)
    bounds = jnp.concatenate(
        [SIDE * jnp.min(coords_f, axis=1), SIDE * jnp.max(coords_f, axis=1) + (SIDE - 1)]
    )
    upward = jnp.einsum("qr,q->r", dev_transfer[0], dev_mom, precision=lax.Precision.HIGHEST)
    all_mom, all_bounds = (
        lax.all_gather(dev_mom[None], "dom", axis=0, tiled=True),
        lax.all_gather(bounds[None], "dom", axis=0, tiled=True),
    )
    group_mom = lax.psum(upward, "dom")
    dev_local = far_coupling(cluster_nodes(bounds), all_bounds, dev_far[0], all_mom)
    group_bounds = jnp.concatenate(
        [jnp.min(all_bounds[:, :3], axis=0), jnp.max(all_bounds[:, 3:], axis=0)]
    )
    coarse_mom, coarse_bounds = (
        lax.all_gather(group_mom[None], "group", axis=0, tiled=True),
        lax.all_gather(group_bounds[None], "group", axis=0, tiled=True),
    )
    group_local = far_coupling(cluster_nodes(group_bounds), coarse_bounds, group_far[0], coarse_mom)
    dev_total = dev_local + jnp.einsum(
        "qr,r->q", dev_transfer[0], group_local, precision=lax.Precision.HIGHEST
    )
    leaf_local = jnp.einsum("lqr,r->lq", leaf_transfer, dev_total, precision=lax.Precision.HIGHEST)
    far_part = jnp.einsum("rlp,lr->lp", leaf_bases, leaf_local, precision=lax.Precision.HIGHEST)
    hartree = (near_part + far_part).reshape(-1)
    return (density, hartree)


def solution(mesh):
    in_specs = (
        P(("group", "dom"), None),
        P(("group", "dom"), None),
        P(("group", "dom"), None),
        P(None, ("group", "dom")),
        P(("group", "dom"), None),
        P(None, ("group", "dom")),
        P(("group", "dom"), None, None),
        P(("group", "dom"), None, None),
        P(("group", "dom"), None),
        P("group", None),
    )
    out_specs = (P(("group", "dom")), P(("group", "dom")))
    return jax.shard_map(local, mesh=mesh, in_specs=in_specs, out_specs=out_specs, check_vma=False)
```

profile of v0, /device:TPU:32, one launch (start us, length us, event | category | flops | bytes accessed | tf_op | source)
XLA Modules:
  0.0 532.1 jit_solution(10032816839666519139)
XLA Ops:
  15.3 4.7 copy.52
  20.5 80.6 %all-gather.6.cloned.1.call-done = bf16[2048,2048]{1,0:T(8,128)(2,1)} async-done(((bf16[32,2048]{1,0:T(8,128)(2,1)}), bf16[2048,2048]{1,0:T(8,128)(2,1)}) %all-gather.6.cloned.1.call-update) | async-done | bytes 8388624 | tf_op jit(solution)/shard_map/all_gather | solution.py:82
  101.1 12.3 %copy.50 = bf16[2048,2048]{0,1:T(8,128)(2,1)} copy(bf16[2048,2048]{1,0:T(8,128)(2,1)} %all-gather.6.cloned.1.call-done) | data formatting | bytes 16777216 | tf_op jit(solution)/shard_map/all_gather | solution.py:82
  113.3 4.1 gather_fusion
  117.4 2.5 copy.51
  119.9 1.8 broadcast_select_fusion
  121.7 2.0 gather_fusion.1
  123.7 5.0 fusion.63
  128.8 5.3 %collective-permute-start.1 = (f32[6,4,512]{2,1,0:T(4,128)S(1)}, f32[6,4,512]{2,1,0:T(4,128)S(1)}, u32[]{:S(2)}, u32[]{:S(2)}) collective-permute-start(f32[6,4,512]{2,1,0:T(4,128)S(1)} %pad_maximum_fusion.1), channel_id=1, source_target_pairs={{1,0},{2,1},{3,2},{4,3},{5,4},{6,5},{7,6},{8,7},{9,8},{10,9},{11,1... | collective-permute-start | bytes 147464 | tf_op jit(solution)/shard_map/ppermute | solution.py:27
  134.1 1.9 collective-permute-start
  137.3 251.2 %all-reduce.3 = (f32[4096]{0:T(1024)S(1)}, f32[384]{0:T(512)S(1)}, f32[1,64]{1,0:T(1,128)S(1)}) all-reduce(f32[4096]{0:T(1024)S(1)} %bitcast_dynamic-update-slice_fusion, f32[384]{0:T(512)S(1)} %maximum_dynamic-update-slice_fusion, f32[1,64]{1,0:T(1,128)S(1)} %fusion.126), channel_id=3, replica_groups=mesh['group'=8,'dom'=64] {'dom'}, use_global_device_ids=true, to_apply=%add.1 | all-reduce | flops 4544 | bytes 36352
  388.6 17.1 %all-gather.3 = f32[8,1,64]{2,1,0:T(1,128)S(1)} all-gather(f32[1,1,64]{2,1,0:T(1,128)S(1)} %bitcast.298), channel_id=1, replica_groups=mesh['group'=8,'dom'=64] {'group'}, dimensions={0}, use_global_device_ids=true | all-gather | bytes 2304 | tf_op jit(solution)/shard_map/all_gather | solution.py:132
  406.2 14.9 %all-reduce.2 = f32[48]{0:T(128)S(1)} all-reduce(f32[48]{0:T(128)S(1)} %maximum_dynamic-update-slice_fusion.1), channel_id=4, replica_groups=mesh['group'=8,'dom'=64] {'group'}, use_global_device_ids=true, to_apply=%add.2 | all-reduce | flops 48 | bytes 384
  427.3 2.6 compare_select_fusion.23
  429.9 2.5 compare_select_fusion.24
  432.4 5.0 compare_select_fusion.11
  437.4 5.0 compare_select_fusion.12
  442.9 2.6 fusion.83
  446.8 77.9 %while.10 = (s32[]{:T(128)}, f32[6,512]{1,0:T(8,128)S(1)}, s32[6]{0:T(128)S(1)}, f32[6,3,512]{2,1,0:T(4,128)S(1)}, s32[6,3]{0,1:T(4,128)S(1)}, /*index=5*/f32[18...) while((s32[]{:T(128)}, f32[6,512]{1,0:T(8,128)S(1)}, ...), condition=%wide.region_2.3_spmd, body=%wide.region_1.2_spmd.sunk | while | flops 16516113 | bytes 110989 | solution.py:113
  455.5 1.4 fusion.172
  456.9 1.4 fusion.174
  458.3 1.4 fusion.173
  469.9 1.4 fusion.174
  471.3 1.4 fusion.173
  482.8 1.4 fusion.174
  484.2 1.4 fusion.173
  495.8 1.4 fusion.174
  497.2 1.4 fusion.173
  508.8 1.4 fusion.174
  510.2 1.4 fusion.173
  521.8 1.4 fusion.174
  523.2 1.4 fusion.173
  (142 shorter events, 31.5 us)
Async XLA Ops:
  7.2 129.6 %copy-start = (f32[6,64,64]{2,1,0:T(8,128)S(1)}, f32[6,64,64]{2,1,0:T(8,128)}, u32[]{:S(2)}) copy-start(f32[6,64,64]{2,1,0:T(8,128)} %param.18) | copy-start | bytes 294916
  7.2 93.9 %all-gather.6.cloned.1.call-start = ((), (), s32[]{:S(2)}) async-start(), calls=%async_computation | async-start | bytes 8519680 | tf_op jit(solution)/shard_map/all_gather | solution.py:82
  15.2 5.1 copy-start.5
  15.2 5.1 copy-start.6
  15.2 5.1 copy-start.7
  123.7 12.3 %copy-start.1 = (f32[64,3072]{1,0:T(8,128)S(1)}, f32[64,3072]{1,0:T(8,128)}, u32[]{:S(2)}) copy-start(f32[64,3072]{1,0:T(8,128)} %param.17) | copy-start | bytes 2359300
  123.7 13.3 %copy-start.2 = (f32[1,64,64]{2,1,0:T(8,128)S(1)}, f32[1,64,64]{2,1,0:T(8,128)}, u32[]{:S(2)}) copy-start(f32[1,64,64]{2,1,0:T(8,128)} %param.19) | copy-start | bytes 49156
  128.7 318.0 %copy-start.3 = (f32[3072]{0:T(1024)}, f32[3072]{0:T(1024)S(1)}, u32[]{:S(2)}) copy-start(f32[3072]{0:T(1024)S(1)} %fusion.63) | copy-start | bytes 36868
  128.8 317.9 %collective-permute-start.1 = (f32[6,4,512]{2,1,0:T(4,128)S(1)}, f32[6,4,512]{2,1,0:T(4,128)S(1)}, u32[]{:S(2)}, u32[]{:S(2)}) collective-permute-start(f32[6,4,512]{2,1,0:T(4,128)S(1)} %pad_maximum_fusion.1), channel_id=1, source_target_pairs={{1,0},{2,1},{3,2},{4,3},{5,4},{6,5},{7,6},{8,7},{9,8},{10,9},{11,1... | collective-permute-start | bytes 147464 | tf_op jit(solution)/shard_map/ppermute | solution.py:27
  134.1 312.6 %collective-permute-start = (f32[6,4,512]{2,1,0:T(4,128)S(1)}, f32[6,4,512]{2,1,0:T(4,128)S(1)}, u32[]{:S(2)}, u32[]{:S(2)}) collective-permute-start(f32[6,4,512]{2,1,0:T(4,128)S(1)} %pad_maximum_fusion.1), channel_id=1, source_target_pairs={{0,1},{1,2},{2,3},{3,4},{4,5},{5,6},{6,7},{7,8},{8,9},{9,10},{10,1... | collective-permute-start | bytes 147464 | tf_op jit(solution)/shard_map/ppermute | solution.py:26
  442.9 3.9 copy-start.4
Sparse Core Ops, SparseCore 0:
  11.4 89.6 all-gather.5
where the time goes:
time: 534 us; the launch traced here: 532 us
  blocking collectives  283 us (53%)
  waiting for transfers between devices  81.2 us (15%)
  loops' own time  45.1 us (8%)
  local copies, waits for them, and re-layouts  43.1 us (8%)
  matrix products  35.3 us (7%)
  other arithmetic  20.4 us (4%)
  between operations  16.4 us (3%)
  starting transfers between devices  7.29 us (1%)
    unnamed x2, blocking collectives  266 us
    all_gather x1, waiting for transfers between devices, local(): row_piece = lax.all_gather(density_rows, 'dom', axis=0, tiled=True)  80.6 us
    another operation x1, loops' own time, local(): near_part = lax.map(near_one, jnp.arange(leaf_count)) * vol_weight  45.1 us
    dot_general x18, matrix products, near_one(): jnp.dot(coulomb(own_points, source_leaf[:3]), source_leaf[3], precision=l...  25 us
    all_gather x1, blocking collectives, local(): lax.all_gather(group_mom[None], 'group', axis=0, tiled=True)  17.1 us
    gather x7, other arithmetic, cluster_nodes(): return jnp.stack([along[0][first], along[1][second], along[2][third]])  15.1 us
    all_gather x1, local copies, waits for them, and re-layouts, local(): row_piece = lax.all_gather(density_rows, 'dom', axis=0, tiled=True)  12.3 us
  transfers between devices with their start and end apart: 3, of which 1 were waited for; matrix products, arithmetic and copies ran while one was open for 7% of the time, Pallas kernels for 0%

commit v1 on v0

v1 whole, which is shorter than its diff:
```python
import functools
import math

import jax
import jax.numpy as jnp
from jax import lax
from jax.experimental import pallas as pl
from jax.experimental.pallas import tpu as pltpu
from jax.sharding import PartitionSpec as P

SIDE = 8
LEAF = 512
CHEB = 4
R = 64
BW = 16
NEAR_B = 32
REACH = 8
LEAVES = 6
NEARL = 3
N_DOM = 64
N_GROUP = 8
ROW = 8
CHUNK = 128
WIDE = 6 * CHUNK

vol_weight = 0.1
MESH = pl.DeviceIdType.MESH
F32 = jnp.float32
BF16 = jnp.bfloat16
CHEB_X = [math.cos((2 * a + 1) * math.pi / (2 * CHEB)) for a in range(CHEB)]


def lanes(start, size):
    return pl.ds(pl.multiple_of(start, size), size)


def remote(src, dst, send, recv, device):
    return pltpu.make_async_remote_copy(
        src_ref=src, dst_ref=dst, send_sem=send, recv_sem=recv, device_id=device, device_id_type=MESH
    )


def signal(barrier, device):
    pl.semaphore_signal(barrier, inc=1, device_id=device, device_id_type=MESH)


def choose(pieces, index):
    piece = pieces[0]
    for s in range(1, ROW):
        piece = jnp.where(index == s, pieces[s], piece)
    return piece


def rows_kernel(
    near, rows, window, hot_rows, stage, first, passed, second, kept,
    w_send, w_recv, h_send, h_recv,
):
    me = lax.axis_index("dom")
    y, j = me // ROW, me % ROW
    barrier = pltpu.get_barrier_semaphore()
    offsets = [s * o for o in range(1, REACH + 1) for s in (1, -1)]
    far_rows = [dy for dy in range(1, ROW) if dy not in (1, ROW - 1)]
    for o in offsets:
        signal(barrier, {"dom": (me + o + N_DOM) % N_DOM})
    for dy in far_rows:
        signal(barrier, {"dom": (me + dy * ROW) % N_DOM})

    hot = near[0, 0] // 2
    base = (me + N_DOM - REACH) // 4
    shared = rows[:, :CHUNK]
    for c in range(1, 16):
        shared = jnp.where(hot // 4 == c, rows[:, c * CHUNK : (c + 1) * CHUNK], shared)
    for kk in range(5):
        for c in range(5):
            chunk = (base + kk + c - 2) % 16
            stage[kk, :, c * CHUNK : (c + 1) * CHUNK] = rows[:, lanes(chunk * CHUNK, CHUNK)]
        stage[kk, :, 5 * CHUNK :] = shared
    window[REACH] = stage[2]
    first[j] = rows[:, lanes(j * 256, 256)]
    pl.semaphore_wait(barrier, len(offsets) + len(far_rows))

    def row_peer(d):
        return {"dom": y * ROW + (j + d) % ROW}

    scatter = []
    for d in range(1, ROW):
        to = (j + d) % ROW
        copy = remote(
            rows.at[:, lanes(to * 256, 256)], first.at[j], h_send.at[0, d], h_recv.at[0, d], row_peer(d)
        )
        copy.start()
        scatter.append(copy)
    wide = []
    for n, o in enumerate(offsets):
        kk = (me + o + N_DOM) // 4 - base
        copy = remote(
            stage.at[kk],
            window.at[REACH - o],
            w_send.at[n],
            w_recv.at[n],
            {"dom": (me + o + N_DOM) % N_DOM},
        )
        copy.start()
        wide.append(copy)
    for copy in scatter:
        copy.wait_recv()
    piece = choose(first, hot % ROW)
    passed[...] = piece
    second[y] = piece
    column = []
    for d in range(1, ROW):
        copy = remote(
            passed, second.at[y], h_send.at[1, d], h_recv.at[1, d], {"dom": (me + d * ROW) % N_DOM}
        )
        copy.start()
        column.append(copy)
    for copy in column:
        copy.wait_recv()
    piece = choose(second, hot // ROW)
    kept[...] = piece
    hot_rows[j] = piece
    gather = []
    for d in range(1, ROW):
        copy = remote(kept, hot_rows.at[j], h_send.at[2, d], h_recv.at[2, d], row_peer(d))
        copy.start()
        gather.append(copy)
    for copy in gather + wide:
        copy.wait_recv()
    for copy in scatter + column + gather + wide:
        copy.wait_send()


def exchange_rows(near_blocks, density_rows):
    return pl.pallas_call(
        rows_kernel,
        out_shape=(
            jax.ShapeDtypeStruct((2 * REACH + 1, 32, WIDE), BF16),
            jax.ShapeDtypeStruct((ROW, 32, 256), BF16),
        ),
        in_specs=[
            pl.BlockSpec(memory_space=pltpu.SMEM),
            pl.BlockSpec(memory_space=pltpu.VMEM),
        ],
        out_specs=(
            pl.BlockSpec(memory_space=pltpu.VMEM),
            pl.BlockSpec(memory_space=pltpu.VMEM),
        ),
        scratch_shapes=[
            pltpu.VMEM((5, 32, WIDE), BF16),
            pltpu.VMEM((ROW, 32, 256), BF16),
            pltpu.VMEM((32, 256), BF16),
            pltpu.VMEM((ROW, 32, 256), BF16),
            pltpu.VMEM((32, 256), BF16),
            pltpu.SemaphoreType.DMA((2 * REACH,)),
            pltpu.SemaphoreType.DMA((2 * REACH,)),
            pltpu.SemaphoreType.DMA((3, ROW)),
            pltpu.SemaphoreType.DMA((3, ROW)),
        ],
        compiler_params=pltpu.CompilerParams(collective_id=0, has_side_effects=True),
    )(near_blocks, density_rows)


def eye64():
    return lax.broadcasted_iota(jnp.int32, (R, R), 0) == lax.broadcasted_iota(jnp.int32, (R, R), 1)


def to_column(row):
    return jnp.sum(jnp.where(eye64(), row, 0.0), axis=1, keepdims=True)


def to_row(column):
    return jnp.sum(jnp.where(eye64(), column, 0.0), axis=0, keepdims=True)


def density_kernel(
    near, coords, place, window, hot_rows, orbitals, basis, transfer, dev_transfer,
    rho_out, message, chosen, local_matrix, moments,
):
    leaf = pl.program_id(0)

    @pl.when(leaf == 0)
    def _():
        me = place[0]
        for k in range(2):
            part = slice(k * BW, (k + 1) * BW)
            for c in range(6):
                chunk = (me // 4 + 14 + c) % 16 if c < 5 else near[0, 0] // 8
                chosen[part, c * CHUNK : (c + 1) * CHUNK] = hot_rows[
                    chunk // 2, part, lanes(chunk % 2 * CHUNK, CHUNK)
                ]
        for k in range(2, NEAR_B):
            block = near[0, k]
            slot = (block // 2 - me + REACH + N_DOM) % N_DOM
            chosen[k * BW : (k + 1) * BW, :] = window[slot, lanes(block % 2 * BW, BW), :]
        lane = lax.broadcasted_iota(jnp.int32, (1, LEAF), 1)
        start = jnp.zeros((1, LEAF), jnp.int32)
        for k in range(NEAR_B):
            block = near[0, k]
            chunk = 5 if k < 2 else (block // 8 - me // 4 + 18) % 16
            start = jnp.where(lane // BW == k, chunk * CHUNK + block % 8 * BW, start)
        start = start + lane % BW
        select = lax.broadcasted_iota(jnp.int32, (WIDE, LEAF), 0) == start
        select = jnp.where(select, 1.0, 0.0).astype(BF16)
        local_matrix[...] = jnp.dot(chosen[...], select, preferred_element_type=F32).astype(BF16)
        moments[...] = jnp.zeros_like(moments)

    values = orbitals[...]
    product = jnp.dot(values, local_matrix[...], preferred_element_type=F32)
    product = product * values.astype(F32)
    folded = (product[:, :128] + product[:, 128:256]) + (product[:, 256:384] + product[:, 384:])
    rho = jnp.sum(folded.T, axis=0, keepdims=True)
    for i in range(4):
        rho_out[pl.ds(leaf * 4 + i, 1), :] = rho[:, i * 128 : (i + 1) * 128]
    leaf_moments = jnp.sum(basis[...] * rho, axis=1, keepdims=True)
    moments[...] += jnp.sum(transfer[0] * leaf_moments, axis=0, keepdims=True)

    @pl.when(leaf == LEAVES - 1)
    def _():
        mine = moments[...]
        upward = jnp.sum(dev_transfer[0] * to_column(mine), axis=0, keepdims=True)
        message[0:1, :] = jnp.concatenate([mine, upward], axis=1)
        lane = lax.broadcasted_iota(jnp.int32, (1, 128), 1)
        packed = jnp.zeros((1, 128), jnp.int32)
        for d in range(3):
            low = high = coords[d, 0]
            for t in range(1, LEAVES):
                low = jnp.minimum(low, coords[d, t])
                high = jnp.maximum(high, coords[d, t])
            packed = jnp.where(lane == d, low, packed)
            packed = jnp.where(lane == 3 + d, high, packed)
            for t in range(LEAVES):
                packed = jnp.where(lane == 8 + 3 * t + d, coords[d, t], packed)
        message[1:2, :] = packed.astype(F32)


def density_and_moments(
    near_blocks, leaf_coords, place, window, hot_rows, orbitals, basis, leaf_transfer, dev_transfer
):
    whole = lambda shape: pl.BlockSpec(shape, lambda t: (0,) * len(shape))
    return pl.pallas_call(
        density_kernel,
        grid=(LEAVES,),
        out_shape=(
            jax.ShapeDtypeStruct((4 * LEAVES, 128), F32),
            jax.ShapeDtypeStruct((2, 128), F32),
        ),
        in_specs=[
            pl.BlockSpec(memory_space=pltpu.SMEM),
            pl.BlockSpec(memory_space=pltpu.SMEM),
            pl.BlockSpec(memory_space=pltpu.SMEM),
            whole((2 * REACH + 1, 32, WIDE)),
            whole((ROW, 32, 256)),
            pl.BlockSpec((LEAF, LEAF), lambda t: (t, 0)),
            pl.BlockSpec((R, LEAF), lambda t: (0, t)),
            pl.BlockSpec((1, R, R), lambda t: (t, 0, 0)),
            whole((1, R, R)),
        ],
        out_specs=(whole((4 * LEAVES, 128)), whole((2, 128))),
        scratch_shapes=[
            pltpu.VMEM((LEAF, WIDE), BF16),
            pltpu.VMEM((LEAF, LEAF), BF16),
            pltpu.VMEM((1, R), F32),
        ],
        compiler_params=pltpu.CompilerParams(vmem_limit_bytes=32 << 20),
    )(near_blocks, leaf_coords, place, window, hot_rows, orbitals, basis, leaf_transfer, dev_transfer)


def moments_kernel(
    rho, message, halo, everyone, domains, mine, total, halo_send, halo_recv, m_send, m_recv
):
    me = lax.axis_index("dom")
    group = lax.axis_index("group")
    y, j = me // ROW, me % ROW
    barrier = pltpu.get_barrier_semaphore()
    before, after = {"dom": (me + N_DOM - 1) % N_DOM}, {"dom": (me + 1) % N_DOM}
    row_peers = [{"dom": y * ROW + (j + d) % ROW} for d in range(1, ROW)]
    column_peers = [{"dom": (me + d * ROW) % N_DOM} for d in range(1, ROW)]
    group_peers = [{"group": (group + d) % N_GROUP} for d in range(1, N_GROUP)]
    peers = row_peers + column_peers + group_peers + [before, after]
    for peer in peers:
        signal(barrier, peer)
    mine[j] = message[...]
    pl.semaphore_wait(barrier, len(peers))

    def send_all(phase, src, dst, targets):
        copies = []
        for d, peer in enumerate(targets):
            copy = remote(src, dst, m_send.at[phase, d], m_recv.at[phase, d], peer)
            copy.start()
            copies.append(copy)
        return copies

    first = send_all(0, message, mine.at[j], row_peers)
    up = remote(rho, halo.at[0], halo_send.at[0], halo_recv.at[0], after)
    up.start()
    down = remote(rho, halo.at[1], halo_send.at[1], halo_recv.at[1], before)
    down.start()
    for copy in first:
        copy.wait_recv()
    everyone[y] = mine[...]
    second = send_all(1, mine, everyone.at[y], column_peers)
    for copy in second:
        copy.wait_recv()
    lane = lax.broadcasted_iota(jnp.int32, (2, 128), 1)
    sums, low, high = (jnp.zeros((2, 128), F32), everyone[0, 0], everyone[0, 0])
    for a in range(ROW):
        for b in range(ROW):
            value = everyone[a, b]
            sums, low, high = (sums + value, jnp.minimum(low, value), jnp.maximum(high, value))
    sums = pltpu.roll(sums, 64, 1)
    is_first = lax.broadcasted_iota(jnp.int32, (2, 128), 0) == 0
    packed = jnp.where(is_first, sums, jnp.where(lane < 3, low, high))
    total[...] = packed
    domains[group] = packed
    third = send_all(2, total, domains.at[group], group_peers)
    for copy in third + [up, down]:
        copy.wait_recv()
    for copy in first + second + third + [up, down]:
        copy.wait_send()


def exchange_moments(rho, message):
    vmem = pl.BlockSpec(memory_space=pltpu.VMEM)
    return pl.pallas_call(
        moments_kernel,
        out_shape=(
            jax.ShapeDtypeStruct((2, 4 * LEAVES, 128), F32),
            jax.ShapeDtypeStruct((ROW, ROW, 2, 128), F32),
            jax.ShapeDtypeStruct((N_GROUP, 2, 128), F32),
        ),
        in_specs=[vmem, vmem],
        out_specs=(vmem, vmem, vmem),
        scratch_shapes=[
            pltpu.VMEM((ROW, 2, 128), F32),
            pltpu.VMEM((2, 128), F32),
            pltpu.SemaphoreType.DMA((2,)),
            pltpu.SemaphoreType.DMA((2,)),
            pltpu.SemaphoreType.DMA((3, ROW)),
            pltpu.SemaphoreType.DMA((3, ROW)),
        ],
        compiler_params=pltpu.CompilerParams(collective_id=1, has_side_effects=True),
    )(rho, message)


def split(value):
    high = value.astype(BF16)
    return high, (value - high.astype(F32)).astype(BF16)


def potential_kernel(
    coords, near_leaves, place, rho, halo, everyone, domains, dev_far, group_far, dev_transfer,
    leaf_transfer, basis, out, rho_rows, sources, spots, table, rows_of, bounds_of, partial,
):
    me = place[0]
    rows_of[...] = jnp.zeros_like(rows_of)
    bounds_of[...] = jnp.zeros_like(bounds_of)
    rows_of[0:N_DOM, :] = everyone[pl.ds(0, N_DOM, stride=2), :]
    bounds_of[0:N_DOM, :] = everyone[pl.ds(1, N_DOM, stride=2), :]
    rows_of[N_DOM : N_DOM + N_GROUP, :] = domains[pl.ds(0, N_GROUP, stride=2), :]
    bounds_of[N_DOM : N_DOM + N_GROUP, :] = domains[pl.ds(1, N_GROUP, stride=2), :]
    mask = jnp.concatenate(
        [dev_far[...], group_far[...], jnp.zeros((1, 128 - N_DOM - N_GROUP), jnp.int32)], axis=1
    ).astype(F32)
    weights = rows_of[...].T[:R, :] * mask
    edges = bounds_of[...].T[:8, :]
    lane = lax.broadcasted_iota(jnp.int32, (1, 128), 1)
    is_dev = lane < N_DOM
    own, other = [], []
    sub = lax.broadcasted_iota(jnp.int32, (8, 128), 0)
    for d in range(3):
        low, high = SIDE * edges[d : d + 1], SIDE * edges[3 + d : 4 + d] + (SIDE - 1)
        first = last = coords[d, 0]
        for t in range(1, LEAVES):
            first = jnp.minimum(first, coords[d, t])
            last = jnp.maximum(last, coords[d, t])
        all_low = jnp.min(jnp.where(is_dev, low, 1e9), axis=1, keepdims=True)
        all_high = jnp.max(jnp.where(is_dev, high, -1e9), axis=1, keepdims=True)
        own_low = jnp.where(is_dev, (SIDE * first).astype(F32), all_low)
        own_high = jnp.where(is_dev, (SIDE * last + (SIDE - 1)).astype(F32), all_high)
        own.append((0.5 * (own_low + own_high), 0.5 * (own_high - own_low)))
        other.append((0.5 * (low + high), 0.5 * (high - low)))

    def pick(index):
        value = jnp.full((8, 128), CHEB_X[0], F32)
        for a in range(1, CHEB):
            value = jnp.where(index == a, CHEB_X[a], value)
        return value

    sites = [[c + h * x for x in CHEB_X] for c, h in own]
    xs = [other[0][0] + other[0][1] * x for x in CHEB_X]
    ys = [other[1][0] + other[1][1] * pick(2 * half + sub // 4) for half in range(2)]
    zs = other[2][0] + other[2][1] * pick(sub % 4)
    dx = [[(s - x) * (s - x) for x in xs] for s in sites[0]]
    dy = [[(s - v) * (s - v) for v in ys] for s in sites[1]]
    dz = [(s - zs) * (s - zs) + 1.0 for s in sites[2]]
    for b in range(CHEB):
        for e in range(CHEB):
            tail = [v + dz[e] for v in dy[b]]
            for a in range(CHEB):
                running = jnp.zeros((8, 128), F32)
                for t in range(8):
                    value = lax.rsqrt(dx[a][t // 2] + tail[t % 2])
                    running = running + value * weights[8 * t : 8 * t + 8]
                r = a * 16 + b * 4 + e
                partial[8 * r : 8 * r + 8, :] = running
    summed = partial[pl.ds(0, R, stride=8), :]
    for k in range(1, 8):
        summed = summed + partial[pl.ds(k, R, stride=8), :]
    summed = summed * vol_weight
    dev_local = jnp.sum(jnp.where(is_dev, summed, 0.0), axis=1, keepdims=True)
    group_local = to_row(jnp.sum(jnp.where(is_dev, 0.0, summed), axis=1, keepdims=True))
    dev_total = to_row(dev_local + jnp.sum(dev_transfer[0] * group_local, axis=1, keepdims=True))

    inside = [jnp.where(me > 0, 1.0, 0.0), 1.0, jnp.where(me < N_DOM - 1, 1.0, 0.0)]
    around = [(me + N_DOM - 1) % N_DOM, me, (me + 1) % N_DOM]
    for s, piece in enumerate((halo[0], rho[...], halo[1])):
        piece = piece * inside[s]
        rho_rows[pl.ds(48 * s, 24, stride=2), :] = piece[:, :64]
        rho_rows[pl.ds(48 * s + 1, 24, stride=2), :] = piece[:, 64:]
        held = everyone[pl.ds(2 * around[s] + 1, 1), :]
        for t in range(LEAVES):
            for d in range(3):
                k = 8 + 3 * t + d
                spots[s * LEAVES + t, d : d + 1, :] = jnp.broadcast_to(held[:, k : k + 1], (1, 128))
    for w in range(3 * LEAVES):
        high, low = split(rho_rows[8 * w : 8 * w + 8, :])
        sources[w] = jnp.concatenate(
            [jnp.concatenate([high, high], axis=1), jnp.concatenate([low, low], axis=1)], axis=0
        )
    q = lax.broadcasted_iota(jnp.int32, (64, 128), 0)
    p = lax.broadcasted_iota(jnp.int32, (64, 128), 1) % 64
    gap_y = (p // 8 - q // 8).astype(F32)
    gap_z = (p % 8 - q % 8).astype(F32)
    step = (2 * sub + lax.broadcasted_iota(jnp.int32, (8, 128), 1) // 64 - 7).astype(F32)

    def one_leaf(t, carry):
        here = spots[LEAVES + t]
        lhs = []
        for n in range(NEARL):
            w = near_leaves[t, n]
            shift = SIDE * (here - spots[w])
            x = step + shift[0:1, :]
            yy, zz = gap_y + shift[1:2, :], gap_z + shift[2:3, :]
            x, flat = x * x, yy * yy + zz * zz + 1.0
            for i in range(8):
                high, low = split(lax.rsqrt(flat + x[i : i + 1, :]))
                table[128 * n : 128 * n + 64, 128 * i : 128 * i + 128] = high
                table[128 * n + 64 : 128 * n + 128, 128 * i : 128 * i + 128] = low
            lhs.append(sources[w])
        both = jnp.dot(jnp.concatenate(lhs, axis=1), table[...], preferred_element_type=F32)
        both = both[:8] + both[8:]
        near = jnp.zeros((1, LEAF), F32)
        for qx in range(SIDE):
            near = near + both[qx : qx + 1, (7 - qx) * 64 : (7 - qx) * 64 + LEAF]
        leaf_local = jnp.sum(leaf_transfer[t] * dev_total, axis=1, keepdims=True)
        far = jnp.sum(basis[:, lanes(t * LEAF, LEAF)] * leaf_local, axis=0, keepdims=True)
        value = near * vol_weight + far
        for i in range(4):
            out[pl.ds(4 * t + i, 1), :] = value[:, 128 * i : 128 * i + 128]
        return carry

    lax.fori_loop(0, LEAVES, one_leaf, 0)


def potential(
    leaf_coords, near_leaves, place, rho, halo, everyone, domains, dev_far, group_far, dev_transfer,
    leaf_transfer, basis,
):
    smem, vmem = pl.BlockSpec(memory_space=pltpu.SMEM), pl.BlockSpec(memory_space=pltpu.VMEM)
    return pl.pallas_call(
        potential_kernel,
        out_shape=jax.ShapeDtypeStruct((4 * LEAVES, 128), F32),
        in_specs=[smem] * 3 + [vmem] * 9,
        out_specs=vmem,
        scratch_shapes=[
            pltpu.VMEM((24 * LEAVES, 64), F32),
            pltpu.VMEM((3 * LEAVES, 16, 128), BF16),
            pltpu.VMEM((3 * LEAVES, 8, 128), F32),
            pltpu.VMEM((128 * NEARL, 1024), BF16),
            pltpu.VMEM((128, 128), F32),
            pltpu.VMEM((128, 128), F32),
            pltpu.VMEM((8 * R, 128), F32),
        ],
        compiler_params=pltpu.CompilerParams(vmem_limit_bytes=32 << 20),
    )(
        leaf_coords, near_leaves, place, rho, halo, everyone, domains, dev_far, group_far,
        dev_transfer, leaf_transfer, basis,
    )


def local(
    orbitals, density_rows, near_blocks, leaf_coords, near_leaves, leaf_basis, leaf_transfer,
    dev_transfer, dev_far, group_far,
):
    place = lax.axis_index("dom").astype(jnp.int32)[None]
    window, hot_rows = exchange_rows(near_blocks, density_rows)
    rho, message = density_and_moments(
        near_blocks, leaf_coords, place, window, hot_rows, orbitals, leaf_basis, leaf_transfer,
        dev_transfer,
    )
    halo, everyone, domains = exchange_moments(rho, message)
    hartree = potential(
        leaf_coords, near_leaves, place, rho, halo, everyone.reshape(2 * N_DOM, 128),
        domains.reshape(2 * N_GROUP, 128), dev_far, group_far, dev_transfer, leaf_transfer,
        leaf_basis,
    )
    return (rho.reshape(-1), hartree.reshape(-1))


def solution(mesh):
    in_specs = (
        P(("group", "dom"), None),
        P(("group", "dom"), None),
        P(("group", "dom"), None),
        P(None, ("group", "dom")),
        P(("group", "dom"), None),
        P(None, ("group", "dom")),
        P(("group", "dom"), None, None),
        P(("group", "dom"), None, None),
        P(("group", "dom"), None),
        P("group", None),
    )
    out_specs = (P(("group", "dom")), P(("group", "dom")))
    return jax.shard_map(local, mesh=mesh, in_specs=in_specs, out_specs=out_specs, check_vma=False)
```

time: 534 us -> 77.7 us (0.15)
  the two profiles are of different devices: /device:TPU:32 before, /device:TPU:1 now
where the time goes in v1:
time: 77.7 us; the launch traced here: 77 us
  Pallas kernels  64.5 us (83%)
  local copies, waits for them, and re-layouts  11.7 us (15%)
    pallas_call x1, Pallas kernels, exchange_rows(): pl.pallas_call(rows_kernel, out_shape=(jax.ShapeDtypeStruct((2 * REACH +...  30 us
    pallas_call x1, Pallas kernels, exchange_moments(): pl.pallas_call(moments_kernel, out_shape=(jax.ShapeDtypeStruct((2, 4 * LE...  22.7 us
    unnamed x41, local copies, waits for them, and re-layouts  11.7 us
    pallas_call x1, Pallas kernels, density_and_moments(): pl.pallas_call(density_kernel, grid=(LEAVES,), out_shape=(jax.ShapeDtypeS...  6.34 us
    pallas_call x1, Pallas kernels, potential(): pl.pallas_call(potential_kernel, out_shape=jax.ShapeDtypeStruct((4 * LEAV...  5.48 us

profile of v1, /device:TPU:1, one launch (start us, length us, event | category | flops | bytes accessed | tf_op | source)
XLA Modules:
  0.0 77.0 jit_solution(5052825893580079616)
XLA Ops:
  0.6 0.0 copy-start.14
  0.6 0.0 copy-start.8
  0.7 0.0 copy-start.19
  0.7 0.0 copy-start.17
  0.7 0.0 copy-start.18
  0.7 30.0 %shard_map.113 = (bf16[17,32,768]{2,1,0:T(8,128)(2,1)}, bf16[8,32,256]{2,1,0:T(8,128)(2,1)}) custom-call(s32[1,32]{1,0:T(1,128)} %near.3, bf16[32,2048]{1,0:T(8,128)(2,1)} %rows.1), custom_call_target="tpu_custom_call" | custom-call | tf_op jit(solution)/shard_map/pallas_call | solution.py:134
  30.7 0.0 copy-start
  30.8 1.9 %copy-done = bf16[3072,512]{1,0:T(8,128)(2,1)S(1)} copy-done((bf16[3072,512]{1,0:T(8,128)(2,1)S(1)}, bf16[3072,512]{1,0:T(8,128)(2,1)}, u32[]{:S(2)}) %copy-start) | copy-done | bytes 3145752
  32.6 1.1 %copy-done.1 = f32[64,3072]{1,0:T(8,128)S(1)} copy-done((f32[64,3072]{1,0:T(8,128)S(1)}, f32[64,3072]{1,0:T(8,128)}, u32[]{:S(2)}) %copy-start.1) | copy-done | bytes 786456
  33.8 1.1 %copy-done.3 = bf16[17,32,768]{2,1,0:T(8,128)(2,1)S(1)} copy-done((bf16[17,32,768]{2,1,0:T(8,128)(2,1)S(1)}, bf16[17,32,768]{2,1,0:T(8,128)(2,1)}, u32[]{:S(2)}) %copy-start.3) | copy-done | bytes 835608
  34.9 0.9 %copy-done.4 = f32[6,64,64]{2,1,0:T(8,128)S(1)} copy-done((f32[6,64,64]{2,1,0:T(8,128)S(1)}, f32[6,64,64]{2,1,0:T(8,128)}, u32[]{:S(2)}) %copy-start.4) | copy-done | bytes 98328
  35.9 0.9 %copy-done.6 = bf16[8,32,256]{2,1,0:T(8,128)(2,1)S(1)} copy-done((bf16[8,32,256]{2,1,0:T(8,128)(2,1)S(1)}, bf16[8,32,256]{2,1,0:T(8,128)(2,1)}, u32[]{:S(2)}) %copy-start.6) | copy-done | bytes 131096
  36.8 0.8 copy-done.7
  37.5 0.7 copy-done.13
  38.2 0.7 copy-done.15
  38.9 6.3 %shard_map.114 = (f32[24,128]{1,0:T(8,128)}, f32[2,128]{1,0:T(2,128)S(1)}) custom-call(s32[1,32]{1,0:T(1,128)S(1)} %copy-done.15, s32[3,6]{1,0:T(4,128)S(1)} %copy-done.13, s32[1]{0:T(128)} %bitcast.place, bf16[17,32,768]{2,1,0:T(8,128)(2,1)S(1)} %copy-done.3, bf16[8,32,256]{2,1,0:T(8,128)(2,1)S(1)} %copy-done.6, bf16[3072,512]{1,0:T(8,128)(2,1)S(1)} %copy-done, ...), custom_call_target="tpu_custom_call" | custom-call | tf_op jit(solution)/shard_map/pallas_call | solution.py:240
  45.2 0.6 copy-done.16
  45.8 22.7 %shard_map.115 = (f32[2,24,128]{2,1,0:T(8,128)}, f32[8,8,2,128]{3,2,1,0:T(2,128)}, f32[8,2,128]{2,1,0:T(2,128)}) custom-call(f32[24,128]{1,0:T(8,128)} %get-tuple-element.11.rho, f32[2,128]{1,0:T(2,128)} %copy-done.16), custom_call_target="tpu_custom_call" | custom-call | tf_op jit(solution)/shard_map/pallas_call | solution.py:324
  68.4 0.0 copy-done.19
  68.4 0.1 copy.12.near_leaves
  68.5 0.0 copy-done.14
  68.5 0.0 copy-done.8
  68.5 0.0 copy-done.17
  68.5 0.0 copy-done.18
  68.6 0.0 copy-done.2
  68.6 0.0 copy-done.5
  68.6 0.0 copy-start.9
  68.6 0.8 %copy-done.9 = f32[8,8,2,128]{3,2,1,0:T(2,128)S(1)} copy-done((f32[8,8,2,128]{3,2,1,0:T(2,128)S(1)}, f32[8,8,2,128]{3,2,1,0:T(2,128)}, u32[]{:S(2)}) %copy-start.9) | copy-done | bytes 65560
  69.4 0.7 copy-done.10
  70.1 0.7 copy-done.11
  70.9 0.7 copy-done.12
  71.6 5.5 %shard_map.116 = f32[24,128]{1,0:T(8,128)} custom-call(s32[3,6]{1,0:T(4,128)S(1)} %copy-done.14, s32[6,3]{1,0:T(8,128)S(1)} %copy.12.near_leaves, s32[1]{0:T(128)} %bitcast.place, f32[24,128]{1,0:T(8,128)S(1)} %copy-done.10, f32[2,24,128]{2,1,0:T(8,128)S(1)} %copy-done.11, f32[128,128]{1,0:T(8,128)S(1)} %bitcast.5, f32[16,128]{1,0:T(8,128)S(1)} %bitcast.7, ...), custom_call_target="tpu_custom_call" | custom-call | tf_op jit(solution)/shard_map/pallas_call | solution.py:470
  (13 shorter events, 0.0 us)
Async XLA Ops:
  0.6 67.9 %copy-start.14 = (s32[3,6]{1,0:T(4,128)S(1)}, s32[3,6]{1,0:T(4,128)}, u32[]{:S(2)}) copy-start(s32[3,6]{1,0:T(4,128)} %coords.3) | copy-start | bytes 220
  0.6 67.9 %copy-start.8 = (f32[1,64,64]{2,1,0:T(8,128)S(1)}, f32[1,64,64]{2,1,0:T(8,128)}, u32[]{:S(2)}) copy-start(f32[1,64,64]{2,1,0:T(8,128)} %dev_transfer.3) | copy-start | bytes 49156
  0.7 67.8 %copy-start.19 = (s32[6,3]{0,1:T(4,128)S(1)}, s32[6,3]{0,1:T(4,128)}, u32[]{:S(2)}) copy-start(s32[6,3]{0,1:T(4,128)} %param.14) | copy-start | bytes 220
  0.7 67.9 %copy-start.17 = (s32[1,64]{1,0:T(1,128)S(1)}, s32[1,64]{1,0:T(1,128)}, u32[]{:S(2)}) copy-start(s32[1,64]{1,0:T(1,128)} %dev_far.1) | copy-start | bytes 772
  0.7 67.9 %copy-start.18 = (s32[1,8]{1,0:T(1,128)S(1)}, s32[1,8]{1,0:T(1,128)}, u32[]{:S(2)}) copy-start(s32[1,8]{1,0:T(1,128)} %group_far.1) | copy-start | bytes 100
  30.7 1.9 %copy-start = (bf16[3072,512]{1,0:T(8,128)(2,1)S(1)}, bf16[3072,512]{1,0:T(8,128)(2,1)}, u32[]{:S(2)}) copy-start(bf16[3072,512]{1,0:T(8,128)(2,1)} %orbitals.1) | copy-start | bytes 9437188
  32.6 1.1 %copy-start.1 = (f32[64,3072]{1,0:T(8,128)S(1)}, f32[64,3072]{1,0:T(8,128)}, u32[]{:S(2)}) copy-start(f32[64,3072]{1,0:T(8,128)} %basis.3) | copy-start | bytes 2359300
  33.8 1.1 %copy-start.3 = (bf16[17,32,768]{2,1,0:T(8,128)(2,1)S(1)}, bf16[17,32,768]{2,1,0:T(8,128)(2,1)}, u32[]{:S(2)}) copy-start(bf16[17,32,768]{2,1,0:T(8,128)(2,1)} %get-tuple-element.9.window) | copy-start | bytes 2506756
  34.9 0.9 %copy-start.4 = (f32[6,64,64]{2,1,0:T(8,128)S(1)}, f32[6,64,64]{2,1,0:T(8,128)}, u32[]{:S(2)}) copy-start(f32[6,64,64]{2,1,0:T(8,128)} %leaf_transfer.1) | copy-start | bytes 294916
  35.8 0.9 %copy-start.6 = (bf16[8,32,256]{2,1,0:T(8,128)(2,1)S(1)}, bf16[8,32,256]{2,1,0:T(8,128)(2,1)}, u32[]{:S(2)}) copy-start(bf16[8,32,256]{2,1,0:T(8,128)(2,1)} %get-tuple-element.10.hot_rows) | copy-start | bytes 393220
  36.8 0.8 copy-start.7
  37.5 0.7 copy-start.13
  38.2 0.7 copy-start.15
  38.9 29.7 %copy-start.2 = (f32[64,3072]{1,0:T(8,128)S(1)}, f32[64,3072]{1,0:T(8,128)}, u32[]{:S(2)}) copy-start(f32[64,3072]{1,0:T(8,128)} %basis.3) | copy-start | bytes 2359300
  38.9 29.7 %copy-start.5 = (f32[6,64,64]{2,1,0:T(8,128)S(1)}, f32[6,64,64]{2,1,0:T(8,128)}, u32[]{:S(2)}) copy-start(f32[6,64,64]{2,1,0:T(8,128)} %leaf_transfer.1) | copy-start | bytes 294916
  45.2 0.6 copy-start.16
  68.6 0.8 %copy-start.9 = (f32[8,8,2,128]{3,2,1,0:T(2,128)S(1)}, f32[8,8,2,128]{3,2,1,0:T(2,128)}, u32[]{:S(2)}) copy-start(f32[8,8,2,128]{3,2,1,0:T(2,128)} %get-tuple-element.14) | copy-start | bytes 196612
  69.4 0.7 copy-start.10
  70.1 0.7 copy-start.11
  70.9 0.7 copy-start.12

commit v2 on v0

v2 whole, which is shorter than its diff:
```python
import functools
import math

import jax
import jax.numpy as jnp
from jax import lax
from jax.experimental import pallas as pl
from jax.experimental.pallas import tpu as pltpu
from jax.sharding import PartitionSpec as P

SIDE = 8
LEAF = 512
CHEB = 4
R = 64
BW = 16
NEAR_B = 32
REACH = 8
LEAVES = 6
NEARL = 3
N_DOM = 64
N_GROUP = 8
ROW = 8
CHUNK = 128
HELD = 2 * REACH + 1
WIDE = 6 * CHUNK

vol_weight = 0.1
MESH = pl.DeviceIdType.MESH
F32 = jnp.float32
BF16 = jnp.bfloat16
CHEB_X = [math.cos((2 * a + 1) * math.pi / (2 * CHEB)) for a in range(CHEB)]


def lanes(start, size):
    return pl.ds(pl.multiple_of(start, size), size)


def remote(src, dst, send, recv, device):
    return pltpu.make_async_remote_copy(
        src_ref=src, dst_ref=dst, send_sem=send, recv_sem=recv, device_id=device, device_id_type=MESH
    )


def signal(barrier, device):
    pl.semaphore_signal(barrier, inc=1, device_id=device, device_id_type=MESH)


def choose(pieces, index):
    piece = pieces[0]
    for s in range(1, len(pieces)):
        piece = jnp.where(index == s, pieces[s], piece)
    return piece


def eye64():
    return lax.broadcasted_iota(jnp.int32, (R, R), 0) == lax.broadcasted_iota(jnp.int32, (R, R), 1)


def to_column(row):
    return jnp.sum(jnp.where(eye64(), row, 0.0), axis=1, keepdims=True)


def to_row(column):
    return jnp.sum(jnp.where(eye64(), column, 0.0), axis=0, keepdims=True)


def split(value):
    high = value.astype(BF16)
    return high, (value - high.astype(F32)).astype(BF16)


def iota(shape, dim):
    return lax.broadcasted_iota(jnp.int32, shape, dim)


def first_and_last(coords, d):
    first = last = coords[d, 0]
    for t in range(1, LEAVES):
        first = jnp.minimum(first, coords[d, t])
        last = jnp.maximum(last, coords[d, t])
    return first, last


def spread(index, shape):
    value = jnp.full(shape, CHEB_X[0], F32)
    for a in range(1, CHEB):
        value = jnp.where(index == a, CHEB_X[a], value)
    return value


def kernel(
    near, coords, near_leaves,
    orbitals_h, rows_h, basis_h, transfer_h, dev_transfer_h, dev_far, group_far,
    rho, out,
    orbitals, rows, basis, transfer, dev_transfer,
    stage, window, first, passed, second, kept, hot_rows,
    meta_row, meta_all, meta_total, meta_groups,
    mom_mine, mom_row, mom_all, mom_total, mom_groups,
    halo, pick_rows, pick_columns, chosen, local_matrix,
    rho_rows, sources, spots, tables, far_rows, far_bounds, couplings, partial,
    load_sem, w_send, w_recv, h_send, h_recv, m_send, m_recv, u_send, u_recv, e_send, e_recv,
):
    me = lax.axis_index("dom")
    group = lax.axis_index("group")
    y, j = me // ROW, me % ROW
    offsets = [s * o for o in range(REACH, 0, -1) for s in (1, -1)]
    far_columns = [dy for dy in range(2, ROW - 1)]
    row_peers = [{"dom": y * ROW + (j + d) % ROW} for d in range(1, ROW)]
    column_peers = [{"dom": (me + d * ROW) % N_DOM} for d in range(1, ROW)]
    group_peers = [{"group": (group + d) % N_GROUP} for d in range(1, N_GROUP)]
    peers = [{"dom": (me + o + N_DOM) % N_DOM} for o in offsets]
    peers = peers + [column_peers[dy - 1] for dy in far_columns] + group_peers
    barrier = pltpu.get_barrier_semaphore()
    for peer in peers:
        signal(barrier, peer)
    loads = []
    for n, (src, dst) in enumerate(
        (
            (rows_h, rows),
            (orbitals_h, orbitals),
            (basis_h, basis),
            (transfer_h, transfer),
            (dev_transfer_h, dev_transfer),
        )
    ):
        copy = pltpu.make_async_copy(src, dst, load_sem.at[n])
        copy.start()
        loads.append(copy)

    def send_all(src, dst, sends, recvs, phase, targets):
        copies = []
        for d, peer in enumerate(targets):
            copy = remote(src, dst, sends.at[phase, d], recvs.at[phase, d], peer)
            copy.start()
            copies.append(copy)
        return copies

    def arrived(copies):
        for copy in copies:
            copy.wait_recv()

    lane = iota((1, 128), 1)
    packed = jnp.zeros((1, 128), jnp.int32)
    for d in range(3):
        low, high = first_and_last(coords, d)
        packed = jnp.where(lane == d, low, packed)
        packed = jnp.where(lane == 3 + d, high, packed)
        for t in range(LEAVES):
            packed = jnp.where(lane == 8 + 3 * t + d, coords[d, t], packed)
    meta_row[j] = packed.astype(F32)

    loads[0].wait()
    hot = near[0, 0] // 2
    base = (me + N_DOM - REACH) // 4
    shared = choose([rows[:, c * CHUNK : (c + 1) * CHUNK] for c in range(16)], hot // 4)
    for kk in range(5):
        for c in range(5):
            chunk = (base + kk + c - 2) % 16
            stage[kk, :, c * CHUNK : (c + 1) * CHUNK] = rows[:, lanes(chunk * CHUNK, CHUNK)]
        stage[kk, :, 5 * CHUNK :] = shared
    window[REACH] = stage[2]
    first[j] = rows[:, lanes(j * 256, 256)]
    pl.semaphore_wait(barrier, len(peers))

    hot_a = []
    for d in range(1, ROW):
        to = (j + d) % ROW
        copy = remote(
            rows.at[:, lanes(to * 256, 256)], first.at[j], h_send.at[0, d - 1], h_recv.at[0, d - 1],
            row_peers[d - 1],
        )
        copy.start()
        hot_a.append(copy)
    meta_a = send_all(meta_row.at[j], meta_row.at[j], m_send, m_recv, 0, row_peers)
    wide = []
    for n, o in enumerate(offsets):
        kk = (me + o + N_DOM) // 4 - base
        copy = remote(stage.at[kk], window.at[REACH - o], w_send.at[n], w_recv.at[n], peers[n])
        copy.start()
        wide.append(copy)

    gap = iota((BW, 640), 1) - iota((BW, 640), 0)
    for k in range(2, NEAR_B):
        block = near[0, k]
        start = (block // 2 - me + REACH + N_DOM) % N_DOM * 32 + block % 2 * BW
        part = jnp.where(gap == start, 1.0, 0.0)[:, : 32 * HELD]
        pick_rows[(k - 2) * BW : (k - 1) * BW, :] = part.astype(BF16)
    wide_lane = iota((1, LEAF), 1)
    start = jnp.zeros((1, LEAF), jnp.int32)
    for k in range(NEAR_B):
        block = near[0, k]
        chunk = 5 if k < 2 else (block // 8 - me // 4 + 18) % 16
        start = jnp.where(wide_lane // BW == k, chunk * CHUNK + block % 8 * BW, start)
    start = start + wide_lane % BW
    pick = jnp.where(iota((WIDE, LEAF), 0) == start, 1.0, 0.0)
    pick_columns[...] = pick.astype(BF16)

    arrived(hot_a)
    piece = choose([first[s] for s in range(ROW)], hot % ROW)
    passed[...] = piece
    second[y] = piece
    hot_b = send_all(passed, second.at[y], h_send, h_recv, 1, column_peers)
    arrived(meta_a)
    meta_all[y] = meta_row[...]
    meta_b = send_all(meta_row, meta_all.at[y], m_send, m_recv, 1, column_peers)
    arrived(hot_b)
    piece = choose([second[s] for s in range(ROW)], hot // ROW)
    kept[...] = piece
    hot_rows[j] = piece
    hot_c = send_all(kept, hot_rows.at[j], h_send, h_recv, 2, row_peers)
    arrived(meta_b)
    low = high = meta_all[0, 0]
    for a in range(ROW):
        for b in range(ROW):
            value = meta_all[a, b]
            low, high = jnp.minimum(low, value), jnp.maximum(high, value)
    bounds = jnp.where(lane < 3, low, high)
    meta_total[...] = bounds
    meta_groups[group] = bounds
    meta_c = send_all(meta_total, meta_groups.at[group], m_send, m_recv, 2, group_peers)

    around = [(me + N_DOM - 1) % N_DOM, me, (me + 1) % N_DOM]
    for s in range(3):
        held = meta_all[around[s] // ROW, around[s] % ROW]
        for t in range(LEAVES):
            for d in range(3):
                k = 8 + 3 * t + d
                spots[s * LEAVES + t, d : d + 1, :] = jnp.broadcast_to(held[:, k : k + 1], (1, 128))
    q = iota((64, 128), 0)
    p = iota((64, 128), 1) % 64
    gap_y = (p // 8 - q // 8).astype(F32)
    gap_z = (p % 8 - q % 8).astype(F32)
    step = (2 * iota((8, 128), 0) + iota((8, 128), 1) // 64 - 7).astype(F32)

    def build(t, carry):
        here = spots[LEAVES + t]
        for n in range(NEARL):
            w = near_leaves[n, t]
            shift = SIDE * (here - spots[w])
            x = step + shift[0:1, :]
            yy, zz = gap_y + shift[1:2, :], gap_z + shift[2:3, :]
            x, flat = x * x, yy * yy + zz * zz + 1.0
            for i in range(8):
                high, low = split(lax.rsqrt(flat + x[i : i + 1, :]))
                tables[t, 128 * n : 128 * n + 64, 128 * i : 128 * i + 128] = high
                tables[t, 128 * n + 64 : 128 * n + 128, 128 * i : 128 * i + 128] = low
        return carry

    lax.fori_loop(0, LEAVES, build, 0)

    for copy in loads[1:]:
        copy.wait()
    arrived(wide)
    arrived(hot_c)
    for c in range(6):
        part = slice(c * CHUNK, (c + 1) * CHUNK)
        if c < 5:
            chunk = (me // 4 + 14 + c) % 16
            chosen[0:32, part] = hot_rows[chunk // 2, :, lanes(chunk % 2 * CHUNK, CHUNK)]
        else:
            options = [
                hot_rows[a, :, b * CHUNK : (b + 1) * CHUNK] for a in range(ROW) for b in range(2)
            ]
            chosen[0:32, part] = choose(options, hot // 4)
    held = window[...].reshape(32 * HELD, WIDE)
    chosen[32:, :] = jnp.dot(pick_rows[...], held, preferred_element_type=F32).astype(BF16)
    matrix = jnp.dot(chosen[...], pick_columns[...], preferred_element_type=F32)
    local_matrix[...] = matrix.astype(BF16)

    def one_density(t, total):
        values = orbitals[pl.ds(pl.multiple_of(t * LEAF, LEAF), LEAF), :]
        product = jnp.dot(values, local_matrix[...], preferred_element_type=F32)
        product = product * values.astype(F32)
        folded = (product[:, :128] + product[:, 128:256]) + (product[:, 256:384] + product[:, 384:])
        here = jnp.sum(folded.T, axis=0, keepdims=True)
        for i in range(4):
            rho[pl.ds(t * 4 + i, 1), :] = here[:, i * 128 : (i + 1) * 128]
        leaf_moments = jnp.sum(basis[:, lanes(t * LEAF, LEAF)] * here, axis=1, keepdims=True)
        return total + jnp.sum(transfer[t] * leaf_moments, axis=0, keepdims=True)

    mine = lax.fori_loop(0, LEAVES, one_density, jnp.zeros((1, R), F32))
    edge = [
        remote(rho, halo.at[0], e_send.at[0], e_recv.at[0], {"dom": around[2]}),
        remote(rho, halo.at[1], e_send.at[1], e_recv.at[1], {"dom": around[0]}),
    ]
    upward = jnp.sum(dev_transfer[0] * to_column(mine), axis=0, keepdims=True)
    mom_mine[...] = jnp.concatenate([mine, upward], axis=1)
    mom_row[j] = mom_mine[...]
    mom_a = send_all(mom_mine, mom_row.at[j], u_send, u_recv, 0, row_peers)
    for copy in edge:
        copy.start()

    arrived(meta_c)
    far_bounds[...] = jnp.zeros_like(far_bounds)
    for a in range(ROW):
        for b in range(ROW):
            far_bounds[a * ROW + b : a * ROW + b + 1, :] = meta_all[a, b]
        far_bounds[N_DOM + a : N_DOM + a + 1, :] = meta_groups[a]
    edges = far_bounds[...].T[:8, :]
    is_dev = lane < N_DOM
    own, other = [], []
    for d in range(3):
        low, high = SIDE * edges[d : d + 1], SIDE * edges[3 + d : 4 + d] + (SIDE - 1)
        dev_low, dev_high = first_and_last(coords, d)
        all_low, all_high = bounds[:, d : d + 1], bounds[:, 3 + d : 4 + d]
        own_low = SIDE * jnp.where(is_dev, dev_low.astype(F32), all_low)
        own_high = SIDE * jnp.where(is_dev, dev_high.astype(F32), all_high) + (SIDE - 1)
        own.append((0.5 * (own_low + own_high), 0.5 * (own_high - own_low)))
        other.append((0.5 * (low + high), 0.5 * (high - low)))
    sub = iota((8, 128), 0)
    sites = [[c + h * x for x in CHEB_X] for c, h in own]
    xs = [other[0][0] + other[0][1] * x for x in CHEB_X]
    ys = [other[1][0] + other[1][1] * spread(2 * half + sub // 4, (8, 128)) for half in range(2)]
    zs = other[2][0] + other[2][1] * spread(sub % 4, (8, 128))
    dx = [[(s - x) * (s - x) for x in xs] for s in sites[0]]
    dy = [[(s - v) * (s - v) for v in ys] for s in sites[1]]
    dz = [(s - zs) * (s - zs) + 1.0 for s in sites[2]]
    for b in range(CHEB):
        for e in range(CHEB):
            rest = [v + dz[e] for v in dy[b]]
            for a in range(CHEB):
                for t in range(8):
                    r = a * 16 + b * 4 + e
                    couplings[r, 8 * t : 8 * t + 8, :] = lax.rsqrt(dx[a][t // 2] + rest[t % 2])

    arrived(mom_a)
    mom_all[y] = mom_row[...]
    mom_b = send_all(mom_row, mom_all.at[y], u_send, u_recv, 1, column_peers)

    arrived(edge)
    inside = [jnp.where(me > 0, 1.0, 0.0), 1.0, jnp.where(me < N_DOM - 1, 1.0, 0.0)]
    for s, held in enumerate((halo[0], rho[...], halo[1])):
        held = held * inside[s]
        rho_rows[pl.ds(48 * s, 24, stride=2), :] = held[:, :64]
        rho_rows[pl.ds(48 * s + 1, 24, stride=2), :] = held[:, 64:]
    for w in range(3 * LEAVES):
        high, low = split(rho_rows[8 * w : 8 * w + 8, :])
        sources[w] = jnp.concatenate(
            [jnp.concatenate([high, high], axis=1), jnp.concatenate([low, low], axis=1)], axis=0
        )

    def one_near(t, carry):
        lhs = jnp.concatenate([sources[near_leaves[n, t]] for n in range(NEARL)], axis=1)
        both = jnp.dot(lhs, tables[t], preferred_element_type=F32)
        both = both[:8] + both[8:]
        value = jnp.zeros((1, LEAF), F32)
        for qx in range(SIDE):
            value = value + both[qx : qx + 1, (7 - qx) * 64 : (7 - qx) * 64 + LEAF]
        for i in range(4):
            out[pl.ds(4 * t + i, 1), :] = value[:, 128 * i : 128 * i + 128] * vol_weight
        return carry

    arrived(mom_b)
    sums = jnp.zeros((1, 128), F32)
    for a in range(ROW):
        for b in range(ROW):
            sums = sums + mom_all[a, b]
    sums = pltpu.roll(sums, 64, 1)
    mom_total[...] = sums
    mom_groups[group] = sums
    mom_c = send_all(mom_total, mom_groups.at[group], u_send, u_recv, 2, group_peers)
    lax.fori_loop(0, LEAVES, one_near, 0)

    arrived(mom_c)
    far_rows[...] = jnp.zeros_like(far_rows)
    for a in range(ROW):
        for b in range(ROW):
            far_rows[a * ROW + b : a * ROW + b + 1, :] = mom_all[a, b]
        far_rows[N_DOM + a : N_DOM + a + 1, :] = mom_groups[a]
    mask = jnp.concatenate(
        [dev_far[...], group_far[...], jnp.zeros((1, 128 - N_DOM - N_GROUP), jnp.int32)], axis=1
    ).astype(F32)
    weights = far_rows[...].T[:R, :] * mask
    for r in range(R):
        running = jnp.zeros((8, 128), F32)
        for t in range(8):
            part = slice(8 * t, 8 * t + 8)
            running = running + couplings[r, part, :] * weights[part]
        partial[8 * r : 8 * r + 8, :] = running
    summed = partial[pl.ds(0, R, stride=8), :]
    for k in range(1, 8):
        summed = summed + partial[pl.ds(k, R, stride=8), :]
    summed = summed * vol_weight
    dev_local = jnp.sum(jnp.where(is_dev, summed, 0.0), axis=1, keepdims=True)
    group_local = to_row(jnp.sum(jnp.where(is_dev, 0.0, summed), axis=1, keepdims=True))
    dev_total = to_row(dev_local + jnp.sum(dev_transfer[0] * group_local, axis=1, keepdims=True))
    for t in range(LEAVES):
        leaf_local = jnp.sum(transfer[t] * dev_total, axis=1, keepdims=True)
        far = jnp.sum(basis[:, t * LEAF : (t + 1) * LEAF] * leaf_local, axis=0, keepdims=True)
        for i in range(4):
            out[4 * t + i : 4 * t + i + 1, :] += far[:, 128 * i : 128 * i + 128]
    for copy in hot_a + hot_b + hot_c + meta_a + meta_b + meta_c + wide:
        copy.wait_send()
    for copy in mom_a + mom_b + mom_c + edge:
        copy.wait_send()


def local(
    orbitals, density_rows, near_blocks, leaf_coords, near_leaves, leaf_basis, leaf_transfer,
    dev_transfer, dev_far, group_far,
):
    smem, vmem = pl.BlockSpec(memory_space=pltpu.SMEM), pl.BlockSpec(memory_space=pltpu.VMEM)
    anywhere = pl.BlockSpec(memory_space=pl.ANY)
    rows = pltpu.VMEM((1, 128), F32)
    eight = pltpu.VMEM((ROW, 1, 128), F32)
    plane = pltpu.VMEM((ROW, ROW, 1, 128), F32)
    sems = pltpu.SemaphoreType.DMA
    density, hartree = pl.pallas_call(
        kernel,
        out_shape=(
            jax.ShapeDtypeStruct((4 * LEAVES, 128), F32),
            jax.ShapeDtypeStruct((4 * LEAVES, 128), F32),
        ),
        in_specs=[smem] * 3 + [anywhere] * 5 + [vmem] * 2,
        out_specs=(vmem, vmem),
        scratch_shapes=[
            pltpu.VMEM((LEAVES * LEAF, LEAF), BF16),
            pltpu.VMEM((32, 16 * CHUNK), BF16),
            pltpu.VMEM((R, LEAVES * LEAF), F32),
            pltpu.VMEM((LEAVES, R, R), F32),
            pltpu.VMEM((1, R, R), F32),
            pltpu.VMEM((5, 32, WIDE), BF16),
            pltpu.VMEM((HELD, 32, WIDE), BF16),
            pltpu.VMEM((ROW, 32, 256), BF16),
            pltpu.VMEM((32, 256), BF16),
            pltpu.VMEM((ROW, 32, 256), BF16),
            pltpu.VMEM((32, 256), BF16),
            pltpu.VMEM((ROW, 32, 256), BF16),
            eight, plane, rows, eight,
            rows, eight, plane, rows, eight,
            pltpu.VMEM((2, 4 * LEAVES, 128), F32),
            pltpu.VMEM((LEAF - 32, 32 * HELD), BF16),
            pltpu.VMEM((WIDE, LEAF), BF16),
            pltpu.VMEM((LEAF, WIDE), BF16),
            pltpu.VMEM((LEAF, LEAF), BF16),
            pltpu.VMEM((24 * LEAVES, 64), F32),
            pltpu.VMEM((3 * LEAVES, 16, 128), BF16),
            pltpu.VMEM((3 * LEAVES, 8, 128), F32),
            pltpu.VMEM((LEAVES, 128 * NEARL, 1024), BF16),
            pltpu.VMEM((128, 128), F32),
            pltpu.VMEM((128, 128), F32),
            pltpu.VMEM((R, R, 128), F32),
            pltpu.VMEM((8 * R, 128), F32),
            sems((5,)),
            sems((2 * REACH,)), sems((2 * REACH,)),
            sems((3, ROW - 1)), sems((3, ROW - 1)),
            sems((3, ROW - 1)), sems((3, ROW - 1)),
            sems((3, ROW - 1)), sems((3, ROW - 1)),
            sems((2,)), sems((2,)),
        ],
        compiler_params=pltpu.CompilerParams(
            collective_id=0, has_side_effects=True, vmem_limit_bytes=60 << 20
        ),
    )(
        near_blocks, leaf_coords, near_leaves.T, orbitals, density_rows, leaf_basis, leaf_transfer,
        dev_transfer, dev_far, group_far,
    )
    return (density.reshape(-1), hartree.reshape(-1))


def solution(mesh):
    in_specs = (
        P(("group", "dom"), None),
        P(("group", "dom"), None),
        P(("group", "dom"), None),
        P(None, ("group", "dom")),
        P(("group", "dom"), None),
        P(None, ("group", "dom")),
        P(("group", "dom"), None, None),
        P(("group", "dom"), None, None),
        P(("group", "dom"), None),
        P("group", None),
    )
    out_specs = (P(("group", "dom")), P(("group", "dom")))
    return jax.shard_map(local, mesh=mesh, in_specs=in_specs, out_specs=out_specs, check_vma=False)
```

time: 534 us -> 56.9 us (0.11)
  the two profiles are of different devices: /device:TPU:32 before, /device:TPU:1 now
where the time goes in v2:
time: 56.9 us; the launch traced here: 56.4 us
  Pallas kernels  53.1 us (93%)
  local copies, waits for them, and re-layouts  2.61 us (5%)
  between operations  0.64 us (1%)
    pallas_call x1, Pallas kernels, local(): pl.pallas_call(kernel, out_shape=(jax.ShapeDtypeStruct((4 * LEAVES, 128),...  53.1 us
    unnamed x2, local copies, waits for them, and re-layouts  2.61 us

profile of v2, /device:TPU:1, one launch (start us, length us, event | category | flops | bytes accessed | tf_op | source)
XLA Modules:
  0.0 56.4 jit_solution(5353181171412163750)
XLA Ops:
  0.6 53.1 %shard_map.113 = (f32[24,128]{1,0:T(8,128)}, f32[24,128]{1,0:T(8,128)}) custom-call(s32[1,32]{1,0:T(1,128)} %near.1, s32[3,6]{1,0:T(4,128)} %coords.1, s32[3,6]{1,0:T(4,128)} %bitcast.5, bf16[3072,512]{1,0:T(8,128)(2,1)} %orbitals_h.1, bf16[32,2048]{1,0:T(8,128)(2,1)} %rows_h.1, f32[64,3072]{1,0:T(8,128)} %basis_h.1, f32[6,64,64]{2,1,0:T(8,128)} %transfer_h.1, ...), custom_call_target="tpu_custom_call" | custom-call | tf_op jit(solution)/shard_map/pallas_call | solution.py:408
  53.8 1.3 %copy.14 = f32[3072]{0:T(1024)} copy(f32[3072]{0:T(1024)} %bitcast.4) | data formatting | bytes 24576
  55.1 1.3 %copy.15 = f32[3072]{0:T(1024)} copy(f32[3072]{0:T(1024)} %bitcast.3) | data formatting | bytes 24576

commit v3 on v2

v3 whole, which is shorter than its diff:
```python
import functools
import math

import jax
import jax.numpy as jnp
from jax import lax
from jax.experimental import pallas as pl
from jax.experimental.pallas import tpu as pltpu
from jax.sharding import PartitionSpec as P

SIDE = 8
LEAF = 512
CHEB = 4
R = 64
BW = 16
NEAR_B = 32
REACH = 8
LEAVES = 6
NEARL = 3
N_DOM = 64
N_GROUP = 8
ROW = 8
FAR_FIRST = (4, 3, 5, 2, 6, 1, 7)
CHUNK = 128
HELD = 2 * REACH + 1
WIDE = 6 * CHUNK

vol_weight = 0.1
MESH = pl.DeviceIdType.MESH
F32 = jnp.float32
BF16 = jnp.bfloat16
CHEB_X = [math.cos((2 * a + 1) * math.pi / (2 * CHEB)) for a in range(CHEB)]


def lanes(start, size):
    return pl.ds(pl.multiple_of(start, size), size)


def remote(src, dst, send, recv, device):
    return pltpu.make_async_remote_copy(
        src_ref=src, dst_ref=dst, send_sem=send, recv_sem=recv, device_id=device, device_id_type=MESH
    )


def signal(barrier, device):
    pl.semaphore_signal(barrier, inc=1, device_id=device, device_id_type=MESH)


def choose(pieces, index):
    piece = pieces[0]
    for s in range(1, len(pieces)):
        piece = jnp.where(index == s, pieces[s], piece)
    return piece


def eye64():
    return lax.broadcasted_iota(jnp.int32, (R, R), 0) == lax.broadcasted_iota(jnp.int32, (R, R), 1)


def to_column(row):
    return jnp.sum(jnp.where(eye64(), row, 0.0), axis=1, keepdims=True)


def to_row(column):
    return jnp.sum(jnp.where(eye64(), column, 0.0), axis=0, keepdims=True)


def split(value):
    high = value.astype(BF16)
    return high, (value - high.astype(F32)).astype(BF16)


def iota(shape, dim):
    return lax.broadcasted_iota(jnp.int32, shape, dim)


def first_and_last(coords, d):
    first = last = coords[d, 0]
    for t in range(1, LEAVES):
        first = jnp.minimum(first, coords[d, t])
        last = jnp.maximum(last, coords[d, t])
    return first, last


def spread(index, shape):
    value = jnp.full(shape, CHEB_X[0], F32)
    for a in range(1, CHEB):
        value = jnp.where(index == a, CHEB_X[a], value)
    return value


def kernel(
    near_h, coords_h, near_leaves_h, group_far_h, dev_far_h,
    orbitals_h, rows_h, basis_h, transfer_h, dev_transfer_h,
    rho_h, out_h, zero_h,
    near, coords, near_leaves, group_far, dev_far,
    orbitals, rows, basis, transfer, dev_transfer, rho, out, zero,
    stage, window, first, passed, second, kept, hot_rows,
    place, places, mom_mine, mom_row, mom_all, mom_total, mom_groups,
    halo, pick_rows, pick_columns, chosen, local_matrix, folded,
    rho_rows, sources, spots, tables, far_rows, far_bounds, partial,
    load_sem, store_sem, w_send, w_recv, h_send, h_recv, u_send, u_recv, e_send, e_recv,
):
    me = lax.axis_index("dom")
    group = lax.axis_index("group")
    y, j = me // ROW, me % ROW
    offsets = [s * o for o in range(REACH, 0, -1) for s in (1, -1)]
    row_peers = [{"dom": y * ROW + (j + d) % ROW} for d in FAR_FIRST]
    column_peers = [{"dom": (me + d * ROW) % N_DOM} for d in FAR_FIRST]
    group_peers = [{"group": (group + d) % N_GROUP} for d in FAR_FIRST]
    peers = [{"dom": (me + o + N_DOM) % N_DOM} for o in offsets]
    peers = peers + [p for d, p in zip(FAR_FIRST, column_peers) if 1 < d < ROW - 1] + group_peers
    barrier = pltpu.get_barrier_semaphore()
    for peer in peers:
        signal(barrier, peer)
    loads = []
    for n, (src, dst) in enumerate(
        (
            (rows_h, rows),
            (near_h, near),
            (coords_h, coords),
            (near_leaves_h, near_leaves),
            (group_far_h, group_far),
            (dev_far_h, dev_far),
            (orbitals_h, orbitals),
            (basis_h, basis),
            (transfer_h, transfer),
            (dev_transfer_h, dev_transfer),
        )
    ):
        loads.append(pltpu.make_async_copy(src, dst, load_sem.at[n]))
    for copy in loads[:6]:
        copy.start()

    def send_all(src, dst, sends, recvs, phase, targets):
        copies = []
        for d, peer in enumerate(targets):
            copy = remote(src, dst, sends.at[phase, d], recvs.at[phase, d], peer)
            copy.start()
            copies.append(copy)
        return copies

    def arrived(copies):
        for copy in copies:
            copy.wait_recv()

    loads[0].wait()
    loads[1].wait()
    hot = near[0, 0] // 2
    base = (me + N_DOM - REACH) // 4
    shared = choose([rows[:, c * CHUNK : (c + 1) * CHUNK] for c in range(16)], hot // 4)
    for kk in range(5):
        for c in range(5):
            chunk = (base + kk + c - 2) % 16
            stage[kk, :, c * CHUNK : (c + 1) * CHUNK] = rows[:, lanes(chunk * CHUNK, CHUNK)]
        stage[kk, :, 5 * CHUNK :] = shared
    window[REACH] = stage[2]
    first[j] = rows[:, lanes(j * 256, 256)]
    loads[2].wait()
    lane = iota((1, 128), 1)
    packed = jnp.zeros((1, 128), jnp.int32)
    for d in range(3):
        low, high = first_and_last(coords, d)
        packed = jnp.where(lane == d, low, packed)
        packed = jnp.where(lane == 3 + d, high, packed)
        for t in range(LEAVES):
            packed = jnp.where(lane == 8 + 3 * t + d, coords[d, t], packed)
    place[...] = packed.astype(F32)
    places[1] = place[...]
    pl.semaphore_wait(barrier, len(peers))

    hot_a = []
    for n, d in enumerate(FAR_FIRST):
        to = (j + d) % ROW
        copy = remote(
            rows.at[:, lanes(to * 256, 256)], first.at[j], h_send.at[0, n], h_recv.at[0, n], row_peers[n]
        )
        copy.start()
        hot_a.append(copy)
    wide = []
    for n, o in enumerate(offsets):
        kk = (me + o + N_DOM) // 4 - base
        copy = remote(stage.at[kk], window.at[REACH - o], w_send.at[n], w_recv.at[n], peers[n])
        copy.start()
        wide.append(copy)
    around = [(me + N_DOM - 1) % N_DOM, me, (me + 1) % N_DOM]
    beside = [
        remote(place, places.at[0], e_send.at[2], e_recv.at[2], {"dom": around[2]}),
        remote(place, places.at[2], e_send.at[3], e_recv.at[3], {"dom": around[0]}),
    ]
    for copy in beside + loads[6:]:
        copy.start()

    gap = iota((BW, 640), 1) - iota((BW, 640), 0)
    for k in range(2, NEAR_B):
        block = near[0, k]
        start = (block // 2 - me + REACH + N_DOM) % N_DOM * 32 + block % 2 * BW
        part = jnp.where(gap == start, 1.0, 0.0)[:, : 32 * HELD]
        pick_rows[(k - 2) * BW : (k - 1) * BW, :] = part.astype(BF16)
    wide_lane = iota((1, LEAF), 1)
    start = jnp.zeros((1, LEAF), jnp.int32)
    for k in range(NEAR_B):
        block = near[0, k]
        chunk = 5 if k < 2 else (block // 8 - me // 4 + 18) % 16
        start = jnp.where(wide_lane // BW == k, chunk * CHUNK + block % 8 * BW, start)
    start = start + wide_lane % BW
    pick = jnp.where(iota((WIDE, LEAF), 0) == start, 1.0, 0.0)
    pick_columns[...] = pick.astype(BF16)

    arrived(hot_a)
    piece = choose([first[s] for s in range(ROW)], hot % ROW)
    passed[...] = piece
    second[y] = piece
    hot_b = send_all(passed, second.at[y], h_send, h_recv, 1, column_peers)
    arrived(hot_b)
    piece = choose([second[s] for s in range(ROW)], hot // ROW)
    kept[...] = piece
    hot_rows[j] = piece
    hot_c = send_all(kept, hot_rows.at[j], h_send, h_recv, 2, row_peers)
    loads[3].wait()
    arrived(beside)
    for s in range(3):
        held = places[s]
        for t in range(LEAVES):
            for d in range(3):
                k = 8 + 3 * t + d
                spots[s * LEAVES + t, d : d + 1, :] = jnp.broadcast_to(held[:, k : k + 1], (1, 128))
    q = iota((64, 128), 0)
    p = iota((64, 128), 1) % 64
    gap_y = (p // 8 - q // 8).astype(F32)
    gap_z = (p % 8 - q % 8).astype(F32)
    step = (2 * iota((8, 128), 0) + iota((8, 128), 1) // 64 - 7).astype(F32)

    def build(t, carry):
        here = spots[LEAVES + t]
        for n in range(NEARL):
            w = near_leaves[n, t]
            shift = SIDE * (here - spots[w])
            x = step + shift[0:1, :]
            yy, zz = gap_y + shift[1:2, :], gap_z + shift[2:3, :]
            x, flat = x * x, yy * yy + zz * zz + 1.0
            for i in range(8):
                high, low = split(lax.rsqrt(flat + x[i : i + 1, :]))
                tables[t, 128 * n : 128 * n + 64, 128 * i : 128 * i + 128] = high
                tables[t, 128 * n + 64 : 128 * n + 128, 128 * i : 128 * i + 128] = low
        return carry

    lax.fori_loop(0, LEAVES, build, 0)

    for copy in loads[4:]:
        copy.wait()
    arrived(wide)
    held = window[...].reshape(32 * HELD, WIDE)
    chosen[...] = jnp.dot(pick_rows[...], held, preferred_element_type=F32).astype(BF16)
    matrix = jnp.dot(chosen[...], pick_columns[...], preferred_element_type=F32)
    local_matrix[0:32, :] = jnp.zeros((32, LEAF), BF16)
    local_matrix[32:, :] = matrix.astype(BF16)

    def window_density(t, carry):
        here = pl.ds(pl.multiple_of(t * LEAF, LEAF), LEAF)
        values = orbitals[here, :]
        product = jnp.dot(values, local_matrix[...], preferred_element_type=F32)
        product = product * values.astype(F32)
        folded[here, :] = (product[:, :128] + product[:, 128:256]) + (
            product[:, 256:384] + product[:, 384:]
        )
        return carry

    lax.fori_loop(0, LEAVES, window_density, 0)

    arrived(hot_c)
    parts = []
    for c in range(5):
        chunk = (me // 4 + 14 + c) % 16
        parts.append(hot_rows[chunk // 2, :, lanes(chunk % 2 * CHUNK, CHUNK)])
    options = [hot_rows[a, :, b * CHUNK : (b + 1) * CHUNK] for a in range(ROW) for b in range(2)]
    parts.append(choose(options, hot // 4))
    matrix = jnp.dot(
        jnp.concatenate(parts, axis=1), pick_columns[...], preferred_element_type=F32
    )
    matrix = jnp.concatenate([matrix, jnp.zeros((96, LEAF), F32)], axis=0).astype(BF16)

    total = jnp.zeros((1, R), F32)
    for t in range(LEAVES):
        here = slice(t * LEAF, (t + 1) * LEAF)
        values = orbitals[here, :]
        product = lax.dot_general(
            values, matrix, (((1,), (1,)), ((), ())), preferred_element_type=F32
        )
        product = product * values[:, :128].astype(F32) + folded[here, :]
        dense = jnp.sum(product.T, axis=0, keepdims=True)
        for i in range(4):
            rho[t * 4 + i : t * 4 + i + 1, :] = dense[:, i * 128 : (i + 1) * 128]
        leaf_moments = jnp.sum(basis[:, here] * dense, axis=1, keepdims=True)
        total = total + jnp.sum(transfer[t] * leaf_moments, axis=0, keepdims=True)
    mine = total
    edge = [
        remote(rho, halo.at[0], e_send.at[0], e_recv.at[0], {"dom": around[2]}),
        remote(rho, halo.at[1], e_send.at[1], e_recv.at[1], {"dom": around[0]}),
    ]
    upward = jnp.sum(dev_transfer[0] * to_column(mine), axis=0, keepdims=True)
    mom_mine[0:1, :] = jnp.concatenate([mine, upward], axis=1)
    mom_mine[1:2, :] = place[...]
    mom_row[j] = mom_mine[...]
    mom_a = send_all(mom_mine, mom_row.at[j], u_send, u_recv, 0, row_peers)
    for copy in edge:
        copy.start()
    rho_store = pltpu.make_async_copy(rho, rho_h, store_sem.at[0])
    rho_store.start()
    zero[...] = jnp.zeros_like(zero)
    zero_store = pltpu.make_async_copy(zero, zero_h, store_sem.at[2])
    zero_store.start()
    arrived(mom_a)
    mom_all[y] = mom_row[...]
    mom_b = send_all(mom_row, mom_all.at[y], u_send, u_recv, 1, column_peers)

    arrived(edge)
    inside = [jnp.where(me > 0, 1.0, 0.0), 1.0, jnp.where(me < N_DOM - 1, 1.0, 0.0)]
    for s, held in enumerate((halo[0], rho[...], halo[1])):
        held = held * inside[s]
        rho_rows[pl.ds(48 * s, 24, stride=2), :] = held[:, :64]
        rho_rows[pl.ds(48 * s + 1, 24, stride=2), :] = held[:, 64:]
    for w in range(3 * LEAVES):
        high, low = split(rho_rows[8 * w : 8 * w + 8, :])
        sources[w] = jnp.concatenate(
            [jnp.concatenate([high, high], axis=1), jnp.concatenate([low, low], axis=1)], axis=0
        )

    def one_near(t, carry):
        lhs = jnp.concatenate([sources[near_leaves[n, t]] for n in range(NEARL)], axis=1)
        both = jnp.dot(lhs, tables[t], preferred_element_type=F32)
        both = both[:8] + both[8:]
        value = jnp.zeros((1, LEAF), F32)
        for qx in range(SIDE):
            value = value + both[qx : qx + 1, (7 - qx) * 64 : (7 - qx) * 64 + LEAF]
        for i in range(4):
            out[pl.ds(4 * t + i, 1), :] = value[:, 128 * i : 128 * i + 128] * vol_weight
        return carry

    lax.fori_loop(0, LEAVES, one_near, 0)

    arrived(mom_b)
    sums, low, high = jnp.zeros((2, 128), F32), mom_all[0, 0], mom_all[0, 0]
    for a in range(ROW):
        for b in range(ROW):
            value = mom_all[a, b]
            sums, low, high = sums + value, jnp.minimum(low, value), jnp.maximum(high, value)
    bounds = jnp.where(lane < 3, low[1:2], high[1:2])
    mom_total[0:1, :] = pltpu.roll(sums, 64, 1)[0:1]
    mom_total[1:2, :] = bounds
    mom_groups[group] = mom_total[...]
    mom_c = send_all(mom_total, mom_groups.at[group], u_send, u_recv, 2, group_peers)

    far_rows[...] = jnp.zeros_like(far_rows)
    far_bounds[...] = jnp.zeros_like(far_bounds)
    for a in range(ROW):
        for b in range(ROW):
            n = a * ROW + b
            far_rows[n : n + 1, :] = mom_all[a, b, 0:1]
            far_bounds[n : n + 1, :] = mom_all[a, b, 1:2]
    mask = jnp.concatenate([dev_far[...], jnp.zeros((1, 128 - N_DOM), jnp.int32)], axis=1)
    weights = far_rows[...].T[:R, :] * mask.astype(F32)
    edges = far_bounds[...].T[:8, :]
    own, other = [], []
    for d in range(3):
        low, high = SIDE * edges[d : d + 1], SIDE * edges[3 + d : 4 + d] + (SIDE - 1)
        own_low, own_high = first_and_last(coords, d)
        own_low = jnp.full((1, 128), SIDE * own_low).astype(F32)
        own_high = jnp.full((1, 128), SIDE * own_high + (SIDE - 1)).astype(F32)
        own.append((0.5 * (own_low + own_high), 0.5 * (own_high - own_low)))
        other.append((0.5 * (low + high), 0.5 * (high - low)))
    sub = iota((8, 128), 0)
    sites = [[c + h * x for x in CHEB_X] for c, h in own]
    xs = [other[0][0] + other[0][1] * x for x in CHEB_X]
    ys = [other[1][0] + other[1][1] * spread(2 * half + sub // 4, (8, 128)) for half in range(2)]
    zs = other[2][0] + other[2][1] * spread(sub % 4, (8, 128))
    dx = [[(s - x) * (s - x) for x in xs] for s in sites[0]]
    dy = [[(s - v) * (s - v) for v in ys] for s in sites[1]]
    dz = [(s - zs) * (s - zs) + 1.0 for s in sites[2]]
    for b in range(CHEB):
        for e in range(CHEB):
            rest = [v + dz[e] for v in dy[b]]
            for a in range(CHEB):
                running = jnp.zeros((8, 128), F32)
                for t in range(8):
                    value = lax.rsqrt(dx[a][t // 2] + rest[t % 2])
                    running = running + value * weights[8 * t : 8 * t + 8]
                r = a * 16 + b * 4 + e
                partial[8 * r : 8 * r + 8, :] = running
    summed = partial[pl.ds(0, R, stride=8), :]
    for k in range(1, 8):
        summed = summed + partial[pl.ds(k, R, stride=8), :]
    dev_local = jnp.sum(summed, axis=1, keepdims=True)
    node = iota((R, 128), 0)
    point = iota((1, 128), 1) % 64
    own_nodes, far_steps = [], []
    for d, scale in enumerate((16, 4, 1)):
        own_low, own_high = SIDE * bounds[:, d : d + 1], SIDE * bounds[:, 3 + d : 4 + d] + (SIDE - 1)
        centre, half = 0.5 * (own_low + own_high), 0.5 * (own_high - own_low)
        own_nodes.append(centre + half * spread(node // scale % 4, (R, 128)))
        far_steps.append(spread(point // scale % 4, (1, 128)))

    arrived(mom_c)
    left = lane < R
    summed = jnp.zeros((R, 128), F32)
    for i in range(N_GROUP // 2):
        one, two = mom_groups[2 * i], mom_groups[2 * i + 1]
        square = jnp.full((R, 128), 1.0, F32)
        for d in range(3):
            low = SIDE * jnp.where(left, one[1:2, d : d + 1], two[1:2, d : d + 1])
            high = jnp.where(left, one[1:2, 3 + d : 4 + d], two[1:2, 3 + d : 4 + d])
            high = SIDE * high + (SIDE - 1)
            gap = own_nodes[d] - (0.5 * (low + high) + 0.5 * (high - low) * far_steps[d])
            square = square + gap * gap
        mask = jnp.where(left, group_far[0, 2 * i], group_far[0, 2 * i + 1]).astype(F32)
        weight = jnp.concatenate([one[0:1, :R], two[0:1, :R]], axis=1) * mask
        summed = summed + lax.rsqrt(square) * weight
    group_local = to_row(jnp.sum(summed, axis=1, keepdims=True))
    dev_total = dev_local + jnp.sum(dev_transfer[0] * group_local, axis=1, keepdims=True)
    dev_total = to_row(dev_total * vol_weight)
    for t in range(LEAVES):
        leaf_local = jnp.sum(transfer[t] * dev_total, axis=1, keepdims=True)
        far = jnp.sum(basis[:, t * LEAF : (t + 1) * LEAF] * leaf_local, axis=0, keepdims=True)
        for i in range(4):
            out[4 * t + i : 4 * t + i + 1, :] += far[:, 128 * i : 128 * i + 128]
    out_store = pltpu.make_async_copy(out, out_h, store_sem.at[1])
    out_store.start()
    for copy in hot_a + hot_b + hot_c + wide + beside + mom_a + mom_b + mom_c + edge:
        copy.wait_send()
    rho_store.wait()
    zero_store.wait()
    out_store.wait()


def local(
    orbitals, density_rows, near_blocks, leaf_coords, near_leaves, leaf_basis, leaf_transfer,
    dev_transfer, dev_far, group_far,
):
    anywhere = pl.BlockSpec(memory_space=pl.ANY)
    rows = pltpu.VMEM((1, 128), F32)
    pair = pltpu.VMEM((2, 128), F32)
    eight = pltpu.VMEM((ROW, 2, 128), F32)
    plane = pltpu.VMEM((ROW, ROW, 2, 128), F32)
    slab = pltpu.VMEM((4 * LEAVES, 128), F32)
    sems = pltpu.SemaphoreType.DMA
    density, hartree, zero = pl.pallas_call(
        kernel,
        out_shape=(jax.ShapeDtypeStruct((4 * LEAVES, 128), F32),) * 3,
        in_specs=[anywhere] * 10,
        out_specs=(anywhere,) * 3,
        scratch_shapes=[
            pltpu.SMEM((1, NEAR_B), jnp.int32),
            pltpu.SMEM((3, LEAVES), jnp.int32),
            pltpu.SMEM((NEARL, LEAVES), jnp.int32),
            pltpu.SMEM((1, N_GROUP), jnp.int32),
            pltpu.VMEM((1, N_DOM), jnp.int32),
            pltpu.VMEM((LEAVES * LEAF, LEAF), BF16),
            pltpu.VMEM((32, 16 * CHUNK), BF16),
            pltpu.VMEM((R, LEAVES * LEAF), F32),
            pltpu.VMEM((LEAVES, R, R), F32),
            pltpu.VMEM((1, R, R), F32),
            slab, slab, slab,
            pltpu.VMEM((5, 32, WIDE), BF16),
            pltpu.VMEM((HELD, 32, WIDE), BF16),
            pltpu.VMEM((ROW, 32, 256), BF16),
            pltpu.VMEM((32, 256), BF16),
            pltpu.VMEM((ROW, 32, 256), BF16),
            pltpu.VMEM((32, 256), BF16),
            pltpu.VMEM((ROW, 32, 256), BF16),
            rows, pltpu.VMEM((3, 1, 128), F32), pair, eight, plane, pair, eight,
            pltpu.VMEM((2, 4 * LEAVES, 128), F32),
            pltpu.VMEM((LEAF - 32, 32 * HELD), BF16),
            pltpu.VMEM((WIDE, LEAF), BF16),
            pltpu.VMEM((LEAF - 32, WIDE), BF16),
            pltpu.VMEM((LEAF, LEAF), BF16),
            pltpu.VMEM((LEAVES * LEAF, 128), F32),
            pltpu.VMEM((24 * LEAVES, 64), F32),
            pltpu.VMEM((3 * LEAVES, 16, 128), BF16),
            pltpu.VMEM((3 * LEAVES, 8, 128), F32),
            pltpu.VMEM((LEAVES, 128 * NEARL, 1024), BF16),
            pltpu.VMEM((128, 128), F32),
            pltpu.VMEM((128, 128), F32),
            pltpu.VMEM((8 * R, 128), F32),
            sems((10,)), sems((3,)),
            sems((2 * REACH,)), sems((2 * REACH,)),
            sems((3, ROW - 1)), sems((3, ROW - 1)),
            sems((3, ROW - 1)), sems((3, ROW - 1)),
            sems((4,)), sems((4,)),
        ],
        compiler_params=pltpu.CompilerParams(
            collective_id=0, has_side_effects=True, vmem_limit_bytes=60 << 20
        ),
    )(
        near_blocks, leaf_coords, near_leaves.T, group_far, dev_far, orbitals, density_rows,
        leaf_basis, leaf_transfer, dev_transfer,
    )
    return ((density + zero).reshape(-1), (hartree + zero).reshape(-1))


def solution(mesh):
    in_specs = (
        P(("group", "dom"), None),
        P(("group", "dom"), None),
        P(("group", "dom"), None),
        P(None, ("group", "dom")),
        P(("group", "dom"), None),
        P(None, ("group", "dom")),
        P(("group", "dom"), None, None),
        P(("group", "dom"), None, None),
        P(("group", "dom"), None),
        P("group", None),
    )
    out_specs = (P(("group", "dom")), P(("group", "dom")))
    return jax.shard_map(local, mesh=mesh, in_specs=in_specs, out_specs=out_specs, check_vma=False)
```

time: 56.9 us -> 52.1 us (0.916)
  Pallas kernels: 53.1 us -> 49.9 us
  local copies, waits for them, and re-layouts: 2.61 us -> 0 us
  other arithmetic: 0 us -> 1.35 us
    pallas_call x1, Pallas kernels: 53.1 us -> 49.9 us  [local(): pl.pallas_call(kernel, out_shape=(jax.ShapeDtypeStruct((4 * LEAVES, 128),...]
    unnamed x2 -> x0, local copies, waits for them, and re-layouts: 2.61 us -> none
    reshape x0 -> x1, other arithmetic: none -> 1.35 us  [local(): return ((density + zero).reshape(-1), (hartree + zero).reshape(-1))]
where the time goes in v3:
time: 52.1 us; the launch traced here: 51.9 us
  Pallas kernels  49.9 us (96%)
  other arithmetic  1.35 us (3%)
  between operations  0.64 us (1%)
    pallas_call x1, Pallas kernels, local(): pl.pallas_call(kernel, out_shape=(jax.ShapeDtypeStruct((4 * LEAVES, 128),...  49.9 us
    reshape x1, other arithmetic, local(): return ((density + zero).reshape(-1), (hartree + zero).reshape(-1))  1.35 us

profile of v3, /device:TPU:1, one launch (start us, length us, event | category | flops | bytes accessed | tf_op | source)
XLA Modules:
  0.0 51.9 jit_solution(14557753952583750915)
XLA Ops:
  0.6 49.9 %shard_map.113 = (f32[24,128]{1,0:T(8,128)}, f32[24,128]{1,0:T(8,128)}, f32[24,128]{1,0:T(8,128)}) custom-call(s32[1,32]{1,0:T(1,128)} %near_h.1, s32[3,6]{1,0:T(4,128)} %coords_h.1, s32[3,6]{1,0:T(4,128)} %bitcast.5, s32[1,8]{1,0:T(1,128)} %group_far_h.1, s32[1,64]{1,0:T(1,128)} %dev_far_h.1, bf16[3072,512]{1,0:T(8,128)(2,1)} %orbitals_h.1, ...), custom_call_target="tpu_custom_call" | custom-call | tf_op jit(solution)/shard_map/pallas_call | solution.py:446
  50.6 1.4 %add_bitcast_fusion = (f32[3072]{0:T(1024)}, f32[3072]{0:T(1024)}) fusion(f32[24,128]{1,0:T(8,128)} %get-tuple-element.7, f32[24,128]{1,0:T(8,128)} %get-tuple-element.6, f32[24,128]{1,0:T(8,128)} %get-tuple-element.5), kind=kLoop, calls=%fused_computation | loop fusion | flops 6144 | bytes 61440 | tf_op jit(solution)/shard_map/reshape | solution.py:497

commit v4 on v3

--- a/solution.py
+++ b/solution.py
@@ -22,7 +22,8 @@
 ROW = 8
 FAR_FIRST = (4, 3, 5, 2, 6, 1, 7)
 CHUNK = 128
-HELD = 2 * REACH + 1
+SPAN = REACH // 2
+HELD = 2 * (2 * SPAN + 1)
 WIDE = 6 * CHUNK
 
 vol_weight = 0.1
@@ -96,19 +97,23 @@
     near, coords, near_leaves, group_far, dev_far,
     orbitals, rows, basis, transfer, dev_transfer, rho, out, zero,
     stage, window, first, passed, second, kept, hot_rows,
-    place, places, mom_mine, mom_row, mom_all, mom_total, mom_groups,
+    place, places, mom_mine, mom_row, bundle, mom_all, mom_total, mom_groups,
     halo, pick_rows, pick_columns, chosen, local_matrix, folded,
-    rho_rows, sources, spots, tables, far_rows, far_bounds, partial,
+    rho_rows, sources, spots, tables, far_rows, partial,
     load_sem, store_sem, w_send, w_recv, h_send, h_recv, u_send, u_recv, e_send, e_recv,
 ):
     me = lax.axis_index("dom")
     group = lax.axis_index("group")
     y, j = me // ROW, me % ROW
-    offsets = [s * o for o in range(REACH, 0, -1) for s in (1, -1)]
+    core, chip = me % 2, me // 2
+    chips = [s * o for o in range(SPAN, 0, -1) for s in (1, -1)]
+    sibling = {"dom": me + 1 - 2 * core}
     row_peers = [{"dom": y * ROW + (j + d) % ROW} for d in FAR_FIRST]
     column_peers = [{"dom": (me + d * ROW) % N_DOM} for d in FAR_FIRST]
     group_peers = [{"group": (group + d) % N_GROUP} for d in FAR_FIRST]
-    peers = [{"dom": (me + o + N_DOM) % N_DOM} for o in offsets]
+    window_peers = [{"dom": (me + 2 * o + N_DOM) % N_DOM} for o in chips]
+    around = [(me + N_DOM - 1) % N_DOM, me, (me + 1) % N_DOM]
+    peers = window_peers + row_peers + [{"dom": around[0]}, {"dom": around[2]}]
     peers = peers + [p for d, p in zip(FAR_FIRST, column_peers) if 1 < d < ROW - 1] + group_peers
     barrier = pltpu.get_barrier_semaphore()
     for peer in peers:
@@ -154,7 +159,7 @@
             chunk = (base + kk + c - 2) % 16
             stage[kk, :, c * CHUNK : (c + 1) * CHUNK] = rows[:, lanes(chunk * CHUNK, CHUNK)]
         stage[kk, :, 5 * CHUNK :] = shared
-    window[REACH] = stage[2]
+    window[2 * SPAN + core] = stage[2]
     first[j] = rows[:, lanes(j * 256, 256)]
     loads[2].wait()
     lane = iota((1, 128), 1)
@@ -178,12 +183,15 @@
         copy.start()
         hot_a.append(copy)
     wide = []
-    for n, o in enumerate(offsets):
-        kk = (me + o + N_DOM) // 4 - base
-        copy = remote(stage.at[kk], window.at[REACH - o], w_send.at[n], w_recv.at[n], peers[n])
+    for n, o in enumerate(chips):
+        kk = (me + 2 * o + N_DOM) // 4 - base
+        slot = 2 * (SPAN - o) + core
+        copy = remote(stage.at[kk], window.at[slot], w_send.at[0, n], w_recv.at[0, n], window_peers[n])
         copy.start()
         wide.append(copy)
-    around = [(me + N_DOM - 1) % N_DOM, me, (me + 1) % N_DOM]
+    own = window.at[2 * SPAN + core]
+    shared_out = [remote(own, own, w_send.at[1, 8], w_recv.at[1, 8], sibling)]
+    shared_out[0].start()
     beside = [
         remote(place, places.at[0], e_send.at[2], e_recv.at[2], {"dom": around[2]}),
         remote(place, places.at[2], e_send.at[3], e_recv.at[3], {"dom": around[0]}),
@@ -191,10 +199,16 @@
     for copy in beside + loads[6:]:
         copy.start()
 
+    arrived(hot_a)
+    piece = choose([first[s] for s in range(ROW)], hot % ROW)
+    passed[...] = piece
+    second[y] = piece
+    hot_b = send_all(passed, second.at[y], h_send, h_recv, 1, column_peers)
     gap = iota((BW, 640), 1) - iota((BW, 640), 0)
     for k in range(2, NEAR_B):
         block = near[0, k]
-        start = (block // 2 - me + REACH + N_DOM) % N_DOM * 32 + block % 2 * BW
+        slot = (block // 4 - chip + SPAN + N_DOM // 2) % (N_DOM // 2) * 2 + block // 2 % 2
+        start = slot * 32 + block % 2 * BW
         part = jnp.where(gap == start, 1.0, 0.0)[:, : 32 * HELD]
         pick_rows[(k - 2) * BW : (k - 1) * BW, :] = part.astype(BF16)
     wide_lane = iota((1, LEAF), 1)
@@ -207,11 +221,6 @@
     pick = jnp.where(iota((WIDE, LEAF), 0) == start, 1.0, 0.0)
     pick_columns[...] = pick.astype(BF16)
 
-    arrived(hot_a)
-    piece = choose([first[s] for s in range(ROW)], hot % ROW)
-    passed[...] = piece
-    second[y] = piece
-    hot_b = send_all(passed, second.at[y], h_send, h_recv, 1, column_peers)
     arrived(hot_b)
     piece = choose([second[s] for s in range(ROW)], hot // ROW)
     kept[...] = piece
@@ -249,7 +258,13 @@
 
     for copy in loads[4:]:
         copy.wait()
-    arrived(wide)
+    for n, o in enumerate(chips):
+        wide[n].wait_recv()
+        piece = window.at[2 * (SPAN - o) + core]
+        copy = remote(piece, piece, w_send.at[1, n], w_recv.at[1, n], sibling)
+        copy.start()
+        shared_out.append(copy)
+    arrived(shared_out)
     held = window[...].reshape(32 * HELD, WIDE)
     chosen[...] = jnp.dot(pick_rows[...], held, preferred_element_type=F32).astype(BF16)
     matrix = jnp.dot(chosen[...], pick_columns[...], preferred_element_type=F32)
@@ -299,8 +314,9 @@
         remote(rho, halo.at[1], e_send.at[1], e_recv.at[1], {"dom": around[0]}),
     ]
     upward = jnp.sum(dev_transfer[0] * to_column(mine), axis=0, keepdims=True)
-    mom_mine[0:1, :] = jnp.concatenate([mine, upward], axis=1)
-    mom_mine[1:2, :] = place[...]
+    beyond = pltpu.roll(place[...], R, 1)
+    mom_mine[0:1, :] = jnp.where(lane < R, jnp.concatenate([mine, mine], axis=1), beyond)
+    mom_mine[1:2, :] = jnp.concatenate([upward, upward], axis=1)
     mom_row[j] = mom_mine[...]
     mom_a = send_all(mom_mine, mom_row.at[j], u_send, u_recv, 0, row_peers)
     for copy in edge:
@@ -311,8 +327,15 @@
     zero_store = pltpu.make_async_copy(zero, zero_h, store_sem.at[2])
     zero_store.start()
     arrived(mom_a)
-    mom_all[y] = mom_row[...]
-    mom_b = send_all(mom_row, mom_all.at[y], u_send, u_recv, 1, column_peers)
+    sums, low, high = jnp.zeros((2, 128), F32), mom_row[0], mom_row[0]
+    for b in range(ROW):
+        value = mom_row[b]
+        bundle[b] = value[0:1]
+        sums, low, high = sums + value, jnp.minimum(low, value), jnp.maximum(high, value)
+    bounds = jnp.where(lane < R + 3, low[0:1], high[0:1])
+    bundle[ROW] = jnp.where(lane < R, sums[1:2], bounds)
+    mom_all[y] = bundle[...]
+    mom_b = send_all(bundle, mom_all.at[y], u_send, u_recv, 1, column_peers)
 
     arrived(edge)
     inside = [jnp.where(me > 0, 1.0, 0.0), 1.0, jnp.where(me < N_DOM - 1, 1.0, 0.0)]
@@ -340,27 +363,23 @@
     lax.fori_loop(0, LEAVES, one_near, 0)
 
     arrived(mom_b)
-    sums, low, high = jnp.zeros((2, 128), F32), mom_all[0, 0], mom_all[0, 0]
+    sums, low, high = jnp.zeros((1, 128), F32), mom_all[0, ROW], mom_all[0, ROW]
     for a in range(ROW):
-        for b in range(ROW):
-            value = mom_all[a, b]
-            sums, low, high = sums + value, jnp.minimum(low, value), jnp.maximum(high, value)
-    bounds = jnp.where(lane < 3, low[1:2], high[1:2])
-    mom_total[0:1, :] = pltpu.roll(sums, 64, 1)[0:1]
-    mom_total[1:2, :] = bounds
+        value = mom_all[a, ROW]
+        sums, low, high = sums + value, jnp.minimum(low, value), jnp.maximum(high, value)
+    bounds = jnp.where(lane < R + 3, low, high)
+    mom_total[...] = jnp.where(lane < R, sums, bounds)
     mom_groups[group] = mom_total[...]
     mom_c = send_all(mom_total, mom_groups.at[group], u_send, u_recv, 2, group_peers)
 
     far_rows[...] = jnp.zeros_like(far_rows)
-    far_bounds[...] = jnp.zeros_like(far_bounds)
     for a in range(ROW):
         for b in range(ROW):
             n = a * ROW + b
-            far_rows[n : n + 1, :] = mom_all[a, b, 0:1]
-            far_bounds[n : n + 1, :] = mom_all[a, b, 1:2]
+            far_rows[n : n + 1, :] = mom_all[a, b]
     mask = jnp.concatenate([dev_far[...], jnp.zeros((1, 128 - N_DOM), jnp.int32)], axis=1)
-    weights = far_rows[...].T[:R, :] * mask.astype(F32)
-    edges = far_bounds[...].T[:8, :]
+    flipped = far_rows[...].T
+    weights, edges = flipped[:R] * mask.astype(F32), flipped[R : R + 8]
     own, other = [], []
     for d in range(3):
         low, high = SIDE * edges[d : d + 1], SIDE * edges[3 + d : 4 + d] + (SIDE - 1)
@@ -395,7 +414,8 @@
     point = iota((1, 128), 1) % 64
     own_nodes, far_steps = [], []
     for d, scale in enumerate((16, 4, 1)):
-        own_low, own_high = SIDE * bounds[:, d : d + 1], SIDE * bounds[:, 3 + d : 4 + d] + (SIDE - 1)
+        own_low, own_high = SIDE * bounds[:, R + d : R + d + 1], bounds[:, R + 3 + d : R + 4 + d]
+        own_high = SIDE * own_high + (SIDE - 1)
         centre, half = 0.5 * (own_low + own_high), 0.5 * (own_high - own_low)
         own_nodes.append(centre + half * spread(node // scale % 4, (R, 128)))
         far_steps.append(spread(point // scale % 4, (1, 128)))
@@ -407,13 +427,14 @@
         one, two = mom_groups[2 * i], mom_groups[2 * i + 1]
         square = jnp.full((R, 128), 1.0, F32)
         for d in range(3):
-            low = SIDE * jnp.where(left, one[1:2, d : d + 1], two[1:2, d : d + 1])
-            high = jnp.where(left, one[1:2, 3 + d : 4 + d], two[1:2, 3 + d : 4 + d])
+            at, to = slice(R + d, R + d + 1), slice(R + 3 + d, R + 4 + d)
+            low = SIDE * jnp.where(left, one[:, at], two[:, at])
+            high = jnp.where(left, one[:, to], two[:, to])
             high = SIDE * high + (SIDE - 1)
             gap = own_nodes[d] - (0.5 * (low + high) + 0.5 * (high - low) * far_steps[d])
             square = square + gap * gap
         mask = jnp.where(left, group_far[0, 2 * i], group_far[0, 2 * i + 1]).astype(F32)
-        weight = jnp.concatenate([one[0:1, :R], two[0:1, :R]], axis=1) * mask
+        weight = jnp.concatenate([one[:, :R], two[:, :R]], axis=1) * mask
         summed = summed + lax.rsqrt(square) * weight
     group_local = to_row(jnp.sum(summed, axis=1, keepdims=True))
     dev_total = dev_local + jnp.sum(dev_transfer[0] * group_local, axis=1, keepdims=True)
@@ -425,7 +446,7 @@
             out[4 * t + i : 4 * t + i + 1, :] += far[:, 128 * i : 128 * i + 128]
     out_store = pltpu.make_async_copy(out, out_h, store_sem.at[1])
     out_store.start()
-    for copy in hot_a + hot_b + hot_c + wide + beside + mom_a + mom_b + mom_c + edge:
+    for copy in hot_a + hot_b + hot_c + wide + shared_out + beside + mom_a + mom_b + mom_c + edge:
         copy.wait_send()
     rho_store.wait()
     zero_store.wait()
@@ -438,9 +459,6 @@
 ):
     anywhere = pl.BlockSpec(memory_space=pl.ANY)
     rows = pltpu.VMEM((1, 128), F32)
-    pair = pltpu.VMEM((2, 128), F32)
-    eight = pltpu.VMEM((ROW, 2, 128), F32)
-    plane = pltpu.VMEM((ROW, ROW, 2, 128), F32)
     slab = pltpu.VMEM((4 * LEAVES, 128), F32)
     sems = pltpu.SemaphoreType.DMA
     density, hartree, zero = pl.pallas_call(
@@ -467,7 +485,14 @@
             pltpu.VMEM((ROW, 32, 256), BF16),
             pltpu.VMEM((32, 256), BF16),
             pltpu.VMEM((ROW, 32, 256), BF16),
-            rows, pltpu.VMEM((3, 1, 128), F32), pair, eight, plane, pair, eight,
+            rows,
+            pltpu.VMEM((3, 1, 128), F32),
+            pltpu.VMEM((2, 128), F32),
+            pltpu.VMEM((ROW, 2, 128), F32),
+            pltpu.VMEM((ROW + 1, 1, 128), F32),
+            pltpu.VMEM((ROW, ROW + 1, 1, 128), F32),
+            rows,
+            pltpu.VMEM((N_GROUP, 1, 128), F32),
             pltpu.VMEM((2, 4 * LEAVES, 128), F32),
             pltpu.VMEM((LEAF - 32, 32 * HELD), BF16),
             pltpu.VMEM((WIDE, LEAF), BF16),
@@ -479,10 +504,9 @@
             pltpu.VMEM((3 * LEAVES, 8, 128), F32),
             pltpu.VMEM((LEAVES, 128 * NEARL, 1024), BF16),
             pltpu.VMEM((128, 128), F32),
-            pltpu.VMEM((128, 128), F32),
             pltpu.VMEM((8 * R, 128), F32),
             sems((10,)), sems((3,)),
-            sems((2 * REACH,)), sems((2 * REACH,)),
+            sems((2, 9)), sems((2, 9)),
             sems((3, ROW - 1)), sems((3, ROW - 1)),
             sems((3, ROW - 1)), sems((3, ROW - 1)),
             sems((4,)), sems((4,)),

time: 52.1 us -> 49.8 us (0.956)
  Pallas kernels: 49.9 us -> 47.4 us
    pallas_call x1, Pallas kernels: 49.9 us -> 47.4 us  [local(): pl.pallas_call(kernel, out_shape=(jax.ShapeDtypeStruct((4 * LEAVES, 128),...]
where the time goes in v4:
time: 49.8 us; the launch traced here: 49.4 us
  Pallas kernels  47.4 us (95%)
  other arithmetic  1.35 us (3%)
  between operations  0.64 us (1%)
    pallas_call x1, Pallas kernels, local(): pl.pallas_call(kernel, out_shape=(jax.ShapeDtypeStruct((4 * LEAVES, 128),...  47.4 us
    reshape x1, other arithmetic, local(): return ((density + zero).reshape(-1), (hartree + zero).reshape(-1))  1.35 us

profile of v4, /device:TPU:1, one launch (start us, length us, event | category | flops | bytes accessed | tf_op | source)
XLA Modules:
  0.0 49.4 jit_solution(4895600728169843665)
XLA Ops:
  0.6 47.4 %shard_map.113 = (f32[24,128]{1,0:T(8,128)}, f32[24,128]{1,0:T(8,128)}, f32[24,128]{1,0:T(8,128)}) custom-call(s32[1,32]{1,0:T(1,128)} %near_h.1, s32[3,6]{1,0:T(4,128)} %coords_h.1, s32[3,6]{1,0:T(4,128)} %bitcast.5, s32[1,8]{1,0:T(1,128)} %group_far_h.1, s32[1,64]{1,0:T(1,128)} %dev_far_h.1, bf16[3072,512]{1,0:T(8,128)(2,1)} %orbitals_h.1, ...), custom_call_target="tpu_custom_call" | custom-call | tf_op jit(solution)/shard_map/pallas_call | solution.py:464
  48.1 1.4 %add_bitcast_fusion = (f32[3072]{0:T(1024)}, f32[3072]{0:T(1024)}) fusion(f32[24,128]{1,0:T(8,128)} %get-tuple-element.7, f32[24,128]{1,0:T(8,128)} %get-tuple-element.6, f32[24,128]{1,0:T(8,128)} %get-tuple-element.5), kind=kLoop, calls=%fused_computation | loop fusion | flops 6144 | bytes 61440 | tf_op jit(solution)/shard_map/reshape | solution.py:521

commit v5 on v4

--- a/solution.py
+++ b/solution.py
@@ -221,6 +221,12 @@
     pick = jnp.where(iota((WIDE, LEAF), 0) == start, 1.0, 0.0)
     pick_columns[...] = pick.astype(BF16)
 
+    for n, o in enumerate(chips):
+        wide[n].wait_recv()
+        piece = window.at[2 * (SPAN - o) + core]
+        copy = remote(piece, piece, w_send.at[1, n], w_recv.at[1, n], sibling)
+        copy.start()
+        shared_out.append(copy)
     arrived(hot_b)
     piece = choose([second[s] for s in range(ROW)], hot // ROW)
     kept[...] = piece
@@ -258,12 +264,6 @@
 
     for copy in loads[4:]:
         copy.wait()
-    for n, o in enumerate(chips):
-        wide[n].wait_recv()
-        piece = window.at[2 * (SPAN - o) + core]
-        copy = remote(piece, piece, w_send.at[1, n], w_recv.at[1, n], sibling)
-        copy.start()
-        shared_out.append(copy)
     arrived(shared_out)
     held = window[...].reshape(32 * HELD, WIDE)
     chosen[...] = jnp.dot(pick_rows[...], held, preferred_element_type=F32).astype(BF16)
@@ -360,7 +360,7 @@
             out[pl.ds(4 * t + i, 1), :] = value[:, 128 * i : 128 * i + 128] * vol_weight
         return carry
 
-    lax.fori_loop(0, LEAVES, one_near, 0)
+    lax.fori_loop(0, LEAVES // 2, one_near, 0)
 
     arrived(mom_b)
     sums, low, high = jnp.zeros((1, 128), F32), mom_all[0, ROW], mom_all[0, ROW]
@@ -419,6 +419,8 @@
         centre, half = 0.5 * (own_low + own_high), 0.5 * (own_high - own_low)
         own_nodes.append(centre + half * spread(node // scale % 4, (R, 128)))
         far_steps.append(spread(point // scale % 4, (1, 128)))
+
+    lax.fori_loop(LEAVES // 2, LEAVES, one_near, 0)
 
     arrived(mom_c)
     left = lane < R

time: 49.8 us -> 48.5 us (0.974)
  Pallas kernels: 47.4 us -> 46.3 us
    pallas_call x1, Pallas kernels: 47.4 us -> 46.3 us  [local(): pl.pallas_call(kernel, out_shape=(jax.ShapeDtypeStruct((4 * LEAVES, 128),...]
where the time goes in v5:
time: 48.5 us; the launch traced here: 48.2 us
  Pallas kernels  46.3 us (95%)
  other arithmetic  1.35 us (3%)
  between operations  0.64 us (1%)
    pallas_call x1, Pallas kernels, local(): pl.pallas_call(kernel, out_shape=(jax.ShapeDtypeStruct((4 * LEAVES, 128),...  46.3 us
    reshape x1, other arithmetic, local(): return ((density + zero).reshape(-1), (hartree + zero).reshape(-1))  1.35 us

profile of v5, /device:TPU:1, one launch (start us, length us, event | category | flops | bytes accessed | tf_op | source)
XLA Modules:
  0.0 48.2 jit_solution(16980844255141350844)
XLA Ops:
  0.6 46.3 %shard_map.113 = (f32[24,128]{1,0:T(8,128)}, f32[24,128]{1,0:T(8,128)}, f32[24,128]{1,0:T(8,128)}) custom-call(s32[1,32]{1,0:T(1,128)} %near_h.1, s32[3,6]{1,0:T(4,128)} %coords_h.1, s32[3,6]{1,0:T(4,128)} %bitcast.5, s32[1,8]{1,0:T(1,128)} %group_far_h.1, s32[1,64]{1,0:T(1,128)} %dev_far_h.1, bf16[3072,512]{1,0:T(8,128)(2,1)} %orbitals_h.1, ...), custom_call_target="tpu_custom_call" | custom-call | tf_op jit(solution)/shard_map/pallas_call | solution.py:466
  46.9 1.4 %add_bitcast_fusion = (f32[3072]{0:T(1024)}, f32[3072]{0:T(1024)}) fusion(f32[24,128]{1,0:T(8,128)} %get-tuple-element.7, f32[24,128]{1,0:T(8,128)} %get-tuple-element.6, f32[24,128]{1,0:T(8,128)} %get-tuple-element.5), kind=kLoop, calls=%fused_computation | loop fusion | flops 6144 | bytes 61440 | tf_op jit(solution)/shard_map/reshape | solution.py:523

commit v6 on v5

--- a/solution.py
+++ b/solution.py
@@ -232,36 +232,6 @@
     kept[...] = piece
     hot_rows[j] = piece
     hot_c = send_all(kept, hot_rows.at[j], h_send, h_recv, 2, row_peers)
-    loads[3].wait()
-    arrived(beside)
-    for s in range(3):
-        held = places[s]
-        for t in range(LEAVES):
-            for d in range(3):
-                k = 8 + 3 * t + d
-                spots[s * LEAVES + t, d : d + 1, :] = jnp.broadcast_to(held[:, k : k + 1], (1, 128))
-    q = iota((64, 128), 0)
-    p = iota((64, 128), 1) % 64
-    gap_y = (p // 8 - q // 8).astype(F32)
-    gap_z = (p % 8 - q % 8).astype(F32)
-    step = (2 * iota((8, 128), 0) + iota((8, 128), 1) // 64 - 7).astype(F32)
-
-    def build(t, carry):
-        here = spots[LEAVES + t]
-        for n in range(NEARL):
-            w = near_leaves[n, t]
-            shift = SIDE * (here - spots[w])
-            x = step + shift[0:1, :]
-            yy, zz = gap_y + shift[1:2, :], gap_z + shift[2:3, :]
-            x, flat = x * x, yy * yy + zz * zz + 1.0
-            for i in range(8):
-                high, low = split(lax.rsqrt(flat + x[i : i + 1, :]))
-                tables[t, 128 * n : 128 * n + 64, 128 * i : 128 * i + 128] = high
-                tables[t, 128 * n + 64 : 128 * n + 128, 128 * i : 128 * i + 128] = low
-        return carry
-
-    lax.fori_loop(0, LEAVES, build, 0)
-
     for copy in loads[4:]:
         copy.wait()
     arrived(shared_out)
@@ -326,6 +296,37 @@
     zero[...] = jnp.zeros_like(zero)
     zero_store = pltpu.make_async_copy(zero, zero_h, store_sem.at[2])
     zero_store.start()
+
+    loads[3].wait()
+    arrived(beside)
+    for s in range(3):
+        held = places[s]
+        for t in range(LEAVES):
+            for d in range(3):
+                k = 8 + 3 * t + d
+                spots[s * LEAVES + t, d : d + 1, :] = jnp.broadcast_to(held[:, k : k + 1], (1, 128))
+    q = iota((64, 128), 0)
+    p = iota((64, 128), 1) % 64
+    gap_y = (p // 8 - q // 8).astype(F32)
+    gap_z = (p % 8 - q % 8).astype(F32)
+    step = (2 * iota((8, 128), 0) + iota((8, 128), 1) // 64 - 7).astype(F32)
+
+    def build(t, carry):
+        here = spots[LEAVES + t]
+        for n in range(NEARL):
+            w = near_leaves[n, t]
+            shift = SIDE * (here - spots[w])
+            x = step + shift[0:1, :]
+            yy, zz = gap_y + shift[1:2, :], gap_z + shift[2:3, :]
+            x, flat = x * x, yy * yy + zz * zz + 1.0
+            for i in range(8):
+                high, low = split(lax.rsqrt(flat + x[i : i + 1, :]))
+                tables[t, 128 * n : 128 * n + 64, 128 * i : 128 * i + 128] = high
+                tables[t, 128 * n + 64 : 128 * n + 128, 128 * i : 128 * i + 128] = low
+        return carry
+
+    lax.fori_loop(0, LEAVES, build, 0)
+
     arrived(mom_a)
     sums, low, high = jnp.zeros((2, 128), F32), mom_row[0], mom_row[0]
     for b in range(ROW):

time: 48.5 us -> 47 us (0.969)
  Pallas kernels: 46.3 us -> 44.8 us
    pallas_call x1, Pallas kernels: 46.3 us -> 44.8 us  [local(): pl.pallas_call(kernel, out_shape=(jax.ShapeDtypeStruct((4 * LEAVES, 128),...]
where the time goes in v6:
time: 47 us; the launch traced here: 46.7 us
  Pallas kernels  44.8 us (95%)
  other arithmetic  1.35 us (3%)
  between operations  0.64 us (1%)
    pallas_call x1, Pallas kernels, local(): pl.pallas_call(kernel, out_shape=(jax.ShapeDtypeStruct((4 * LEAVES, 128),...  44.8 us
    reshape x1, other arithmetic, local(): return ((density + zero).reshape(-1), (hartree + zero).reshape(-1))  1.35 us

profile of v6, /device:TPU:1, one launch (start us, length us, event | category | flops | bytes accessed | tf_op | source)
XLA Modules:
  0.0 46.7 jit_solution(1361716665997863730)
XLA Ops:
  0.6 44.8 %shard_map.113 = (f32[24,128]{1,0:T(8,128)}, f32[24,128]{1,0:T(8,128)}, f32[24,128]{1,0:T(8,128)}) custom-call(s32[1,32]{1,0:T(1,128)} %near_h.1, s32[3,6]{1,0:T(4,128)} %coords_h.1, s32[3,6]{1,0:T(4,128)} %bitcast.5, s32[1,8]{1,0:T(1,128)} %group_far_h.1, s32[1,64]{1,0:T(1,128)} %dev_far_h.1, bf16[3072,512]{1,0:T(8,128)(2,1)} %orbitals_h.1, ...), custom_call_target="tpu_custom_call" | custom-call | tf_op jit(solution)/shard_map/pallas_call | solution.py:467
  45.4 1.4 %add_bitcast_fusion = (f32[3072]{0:T(1024)}, f32[3072]{0:T(1024)}) fusion(f32[24,128]{1,0:T(8,128)} %get-tuple-element.7, f32[24,128]{1,0:T(8,128)} %get-tuple-element.6, f32[24,128]{1,0:T(8,128)} %get-tuple-element.5), kind=kLoop, calls=%fused_computation | loop fusion | flops 6144 | bytes 61440 | tf_op jit(solution)/shard_map/reshape | solution.py:524

commit v7 on v6

--- a/solution.py
+++ b/solution.py
@@ -325,7 +325,7 @@
                 tables[t, 128 * n + 64 : 128 * n + 128, 128 * i : 128 * i + 128] = low
         return carry
 
-    lax.fori_loop(0, LEAVES, build, 0)
+    lax.fori_loop(0, LEAVES // 2, build, 0)
 
     arrived(mom_a)
     sums, low, high = jnp.zeros((2, 128), F32), mom_row[0], mom_row[0]
@@ -362,6 +362,7 @@
         return carry
 
     lax.fori_loop(0, LEAVES // 2, one_near, 0)
+    lax.fori_loop(LEAVES // 2, LEAVES, build, 0)
 
     arrived(mom_b)
     sums, low, high = jnp.zeros((1, 128), F32), mom_all[0, ROW], mom_all[0, ROW]

time: 47 us -> 47 us (level)
  no operation moved by 1% of the time
where the time goes in v7:
time: 47 us; the launch traced here: 46.7 us
  Pallas kernels  44.8 us (95%)
  other arithmetic  1.35 us (3%)
  between operations  0.64 us (1%)
    pallas_call x1, Pallas kernels, local(): pl.pallas_call(kernel, out_shape=(jax.ShapeDtypeStruct((4 * LEAVES, 128),...  44.8 us
    reshape x1, other arithmetic, local(): return ((density + zero).reshape(-1), (hartree + zero).reshape(-1))  1.35 us

profile of v7, /device:TPU:1, one launch (start us, length us, event | category | flops | bytes accessed | tf_op | source)
XLA Modules:
  0.0 46.7 jit_solution(8440610502046581944)
XLA Ops:
  0.6 44.8 %shard_map.113 = (f32[24,128]{1,0:T(8,128)}, f32[24,128]{1,0:T(8,128)}, f32[24,128]{1,0:T(8,128)}) custom-call(s32[1,32]{1,0:T(1,128)} %near_h.1, s32[3,6]{1,0:T(4,128)} %coords_h.1, s32[3,6]{1,0:T(4,128)} %bitcast.5, s32[1,8]{1,0:T(1,128)} %group_far_h.1, s32[1,64]{1,0:T(1,128)} %dev_far_h.1, bf16[3072,512]{1,0:T(8,128)(2,1)} %orbitals_h.1, ...), custom_call_target="tpu_custom_call" | custom-call | tf_op jit(solution)/shard_map/pallas_call | solution.py:468
  45.4 1.4 %add_bitcast_fusion = (f32[3072]{0:T(1024)}, f32[3072]{0:T(1024)}) fusion(f32[24,128]{1,0:T(8,128)} %get-tuple-element.7, f32[24,128]{1,0:T(8,128)} %get-tuple-element.6, f32[24,128]{1,0:T(8,128)} %get-tuple-element.5), kind=kLoop, calls=%fused_computation | loop fusion | flops 6144 | bytes 61440 | tf_op jit(solution)/shard_map/reshape | solution.py:525
